TPU v7x, 32 devices: a whole 2x2x4 slice. The times are simulated.
32 devices in a mesh: gx: 8 (over z, core), gy: 4 (over y, x).
Axes of the slice: x: 2, y: 2, z: 4, core: 2. Of those that a mesh axis runs over, the one named last changes fastest.
Arguments:
- terminal: float32 [2048, 2048], P('gx', 'gy'), may hold values from -6 to 6
- crowding: float32 [2048, 2048], P('gx', 'gy'), may hold values from 0.5 to 4
- density: float32 [2048, 2048], P('gx', 'gy'), may hold values from 0.25 to 36, as said below
- fractions: float32 [4, 2, 2048, 2048], P(None, None, 'gx', 'gy'), may hold values from 0 to 1
- offsets: int32 [4, 8, 2], replicated, may hold values from -64 to 63
- control_cost: float32 [4, 8], replicated, may hold values from 0 to 4
Outputs:
- value_start: float32 [2048, 2048], P('gx', 'gy')
- density_end: float32 [2048, 2048], P('gx', 'gy')
- masses: float32 [4], replicated
Inputs may be any that keep to these rules, and one draw needn't show every extreme that they name: `density`: positive.
All inputs are finite; a program needn't handle non-finite values.
Results may differ from a plain program's by a relative error of at most 0.0001.
Values sent between devices are 32-bit elements; how exact they have to be, the bound alone decides.
No kernel may reach another device: no remote copies, remote signals or barrier semaphores. Data moves between devices by JAX's collectives and lax.ppermute only.
A program may use at most 128 MiB of HBM per device.

v0:
```python
from functools import reduce

import jax
import jax.numpy as jnp
from jax import lax
from jax.sharding import PartitionSpec as P

REACH = 64


time_step = 0.1
temper = 0.3
epsilon = 1e-06


def with_halo(cells, sides, width):
    for axis, dim in sides:
        count = lax.axis_size(axis)
        head = lax.slice_in_dim(cells, 0, width, axis=dim)
        tail = lax.slice_in_dim(cells, cells.shape[dim] - width, cells.shape[dim], axis=dim)
        cells = jnp.concatenate(
            [
                lax.ppermute(tail, axis, [(i, (i + 1) % count) for i in range(count)]),
                cells,
                lax.ppermute(head, axis, [((i + 1) % count, i) for i in range(count)]),
            ],
            axis=dim,
        )
    return cells


def catmull(fraction):
    square = fraction * fraction
    cube = square * fraction
    return [
        (-cube + 2.0 * square - fraction) * 0.5,
        (3.0 * cube - 5.0 * square + 2.0) * 0.5,
        (-3.0 * cube + 4.0 * square + fraction) * 0.5,
        (cube - square) * 0.5,
    ]


def sample(padded, weights_x, weights_y, shift_row, shift_col, margin, height, breadth):
    summed = None
    for row_tap in range(4):
        partial_sum = None
        for col_tap in range(4):
            piece = lax.dynamic_slice(
                padded,
                (margin + shift_row + row_tap - 1, margin + shift_col + col_tap - 1),
                (height, breadth),
            )
            term = weights_y[col_tap] * piece
            partial_sum = term if partial_sum is None else partial_sum + term
        term = weights_x[row_tap] * partial_sum
        summed = term if summed is None else summed + term
    return summed


def option_values(
    padded, weights_x, weights_y, offsets, control_cost, crowding, moment, margin, height, breadth
):
    candidates = []
    for option in range(offsets.shape[1]):
        shifted = sample(
            padded,
            weights_x,
            weights_y,
            offsets[moment, option, 0],
            offsets[moment, option, 1],
            margin,
            height,
            breadth,
        )
        candidates.append(shifted + time_step * (control_cost[moment, option] + crowding))
    return candidates


def policy(candidates):
    lowest = reduce(jnp.minimum, candidates)
    ramps = [jnp.maximum(lowest + temper - candidate, 0.0) for candidate in candidates]
    ramp_sum = reduce(jnp.add, ramps)
    return (lowest, [ramp / ramp_sum for ramp in ramps])


def shards(terminal, crowding, density, fractions, offsets, control_cost):
    margin = REACH + 2
    height, breadth = terminal.shape
    steps_count = fractions.shape[0]
    controls_count = offsets.shape[1]
    cells = height * breadth * lax.axis_size("gx") * lax.axis_size("gy")
    current_value = terminal
    policies = [None] * steps_count
    stored = [None] * steps_count
    for moment in reversed(range(steps_count)):
        padded = with_halo(current_value, (("gx", 0), ("gy", 1)), margin)
        weights_x = catmull(fractions[moment, 0])
        weights_y = catmull(fractions[moment, 1])
        candidates = option_values(
            padded,
            weights_x,
            weights_y,
            offsets,
            control_cost,
            crowding,
            moment,
            margin,
            height,
            breadth,
        )
        stored[moment] = current_value
        current_value, policies[moment] = policy(candidates)
    current = density
    local_sums = []
    for moment in range(steps_count):
        weights_x = catmull(fractions[moment, 0])
        weights_y = catmull(fractions[moment, 1])
        weights_now = policies[moment]
        padded = with_halo(current, (("gx", 0), ("gy", 1)), margin)
        arrived = None
        for option in range(controls_count):
            shifted = sample(
                padded,
                weights_x,
                weights_y,
                -offsets[moment, option, 0],
                -offsets[moment, option, 1],
                margin,
                height,
                breadth,
            )
            term = weights_now[option] * shifted
            arrived = term if arrived is None else arrived + term
        arrived = jnp.maximum(arrived, 0.0)
        local_sums.append(jnp.sum(arrived))
        current = arrived
    totals = lax.psum(jnp.stack(local_sums), ("gx", "gy")) / cells
    masses = jnp.concatenate([totals[:1], totals[1:] / totals[:-1]])
    current = current / (totals[-1] + epsilon)
    return (current_value, current, masses)


def solution(mesh):
    return jax.shard_map(
        shards,
        mesh=mesh,
        in_specs=(P("gx", "gy"), P("gx", "gy"), P("gx", "gy"), P(None, None, "gx", "gy"), P(), P()),
        out_specs=(P("gx", "gy"), P("gx", "gy"), P()),
        check_vma=False,
    )
```

profile of v0, /device:TPU:0, one launch (start us, length us, event | category | flops | bytes accessed | tf_op | source)
XLA Modules:
  0.0 835.6 jit_solution(6059356283751571399)
XLA Ops:
  0.6 1.1 fusion.114
  2.3 4.1 collective-permute-start.1
  6.3 1.8 fusion.118
  63.6 1.5 fusion.119
  90.0 2.0 collective-permute-start.2
  92.0 1.0 collective-permute-start.3
  93.7 4.9 collective-permute-done.2
  98.6 2.2 collective-permute-done.3
  101.2 30.2 %minimum_minimum_fusion.5 = (f32[256,512]{1,0:T(8,128)S(1)}, f32[256,512]{1,0:T(8,128)}, f32[256,512]{1,0:T(8,128)}, f32[256,512]{1,0:T(8,128)}, f32[256,512]{1,...) fusion(f32[256,512]{1,0:T(8,128)S(1)} %copy-done, ...), kind=kLoop, calls=%fused_computation.186 | loop fusion | flops 45744128 | bytes 73400608 | tf_op jit(solution)/shard_map/min | solution.py:80
  131.6 3.5 collective-permute-start.5
  216.1 1.5 collective-permute-start.6
  217.7 1.6 collective-permute-start.7
  220.0 4.3 collective-permute-done.6
  224.3 1.2 collective-permute-done.7
  225.9 31.2 %minimum_minimum_fusion.3 = (f32[256,512]{1,0:T(8,128)S(1)}, f32[256,512]{1,0:T(8,128)}, f32[256,512]{1,0:T(8,128)}, f32[256,512]{1,0:T(8,128)}, f32[256,512]{1,...) fusion(f32[256,512]{1,0:T(8,128)S(1)} %copy-done, ...), kind=kLoop, calls=%fused_computation.176 | loop fusion | flops 45744128 | bytes 73400608 | tf_op jit(solution)/shard_map/min | solution.py:80
  257.2 3.5 collective-permute-start.9
  261.5 3.5 collective-permute-start.17
  317.2 1.5 collective-permute-start.10
  318.8 1.8 collective-permute-start.11
  444.6 30.9 %minimum_minimum_fusion.1 = (f32[256,512]{1,0:T(8,128)S(1)}, f32[256,512]{1,0:T(8,128)}, f32[256,512]{1,0:T(8,128)}, f32[256,512]{1,0:T(8,128)}, f32[256,512]{1,...) fusion(f32[256,512]{1,0:T(8,128)S(1)} %copy-done, ...), kind=kLoop, calls=%fused_computation.166 | loop fusion | flops 45744128 | bytes 73400608 | tf_op jit(solution)/shard_map/min | solution.py:80
  475.6 3.5 collective-permute-start.13
  480.0 2.3 collective-permute-start.19
  482.8 2.8 collective-permute-start.15
  485.6 2.6 collective-permute-done.18
  488.1 4.4 collective-permute-done.19
  492.9 2.0 collective-permute-done.14
  494.9 2.2 collective-permute-done.15
  497.2 1.4 pad_maximum_fusion.3
  498.6 145.6 %fusion.104 = (f32[]{:T(128)}, f32[256,512]{1,0:T(8,128)S(1)}, f32[256,512]{1,0:T(8,128)}) fusion(f32[388,644]{1,0:T(8,128)S(1)} %pad_maximum_fusion.4, s32[]{:T(128)S(6)} %select_n.1343, s32[]{:T(128)S(6)} %select_n.1340, s32[]{:T(128)S(6)} %select_n.1339, s32[]{:T(128)S(6)} %select_n.1338, s32[]{:T(128)S(6)} %select_n.1337, s32[]{:T(128)S(6)} %select_n.1342, ...), kind=kLoop, calls=%fused_computation.224 | loop fusion | flops 88866816 | bytes 136839712 | tf_op jit(solution)/shard_map/reduce_sum | solution.py:135
  644.2 3.5 collective-permute-start.21
  647.8 2.8 collective-permute-done.20
  652.0 2.3 collective-permute-start.23
  665.3 1.5 pad_maximum_fusion.5
  666.9 26.1 %fusion.105 = (f32[]{:T(128)}, f32[256,512]{1,0:T(8,128)S(1)}) fusion(f32[388,644]{1,0:T(8,128)S(1)} %pad_maximum_fusion.5, s32[]{:T(128)S(6)} %select_n.1407, s32[]{:T(128)S(6)} %select_n.1404, s32[]{:T(128)S(6)} %select_n.1403, s32[]{:T(128)S(6)} %select_n.1402, s32[]{:T(128)S(6)} %select_n.1401, s32[]{:T(128)S(6)} %select_n.1406, s32[]{:T(128)S(6)} %select_n.1405, ...), kind=kLoop, calls=%fused_computation.225 | loop fusion | flops 49020928 | bytes 72876288 | tf_op jit(solution)/shard_map/reduce_sum | solution.py:135
  693.1 3.5 collective-permute-start.25
  696.6 4.3 collective-permute-done.24
  701.8 3.1 collective-permute-start.27
  715.5 1.6 pad_maximum_fusion.6
  717.1 26.2 %fusion.106 = (f32[]{:T(128)}, f32[256,512]{1,0:T(8,128)S(1)}) fusion(f32[388,644]{1,0:T(8,128)S(1)} %pad_maximum_fusion.6, s32[]{:T(128)S(6)} %select_n.1471, s32[]{:T(128)S(6)} %select_n.1468, s32[]{:T(128)S(6)} %select_n.1467, s32[]{:T(128)S(6)} %select_n.1466, s32[]{:T(128)S(6)} %select_n.1465, s32[]{:T(128)S(6)} %select_n.1470, s32[]{:T(128)S(6)} %select_n.1469, ...), kind=kLoop, calls=%fused_computation.226 | loop fusion | flops 49020928 | bytes 72876288 | tf_op jit(solution)/shard_map/reduce_sum | solution.py:135
  743.4 3.5 collective-permute-start.29
  746.9 3.1 collective-permute-done.28
  750.9 3.2 collective-permute-start.31
  764.6 1.6 pad_maximum_fusion.7
  766.3 25.9 %fusion.107 = (f32[]{:T(128)}, f32[256,512]{1,0:T(8,128)S(1)}) fusion(f32[388,644]{1,0:T(8,128)S(1)} %pad_maximum_fusion.7, s32[]{:T(128)S(6)} %select_n.1535, s32[]{:T(128)S(6)} %select_n.1532, s32[]{:T(128)S(6)} %select_n.1531, s32[]{:T(128)S(6)} %select_n.1530, s32[]{:T(128)S(6)} %select_n.1529, s32[]{:T(128)S(6)} %select_n.1534, s32[]{:T(128)S(6)} %select_n.1533, ...), kind=kLoop, calls=%fused_computation.227 | loop fusion | flops 49020928 | bytes 72876288 | tf_op jit(solution)/shard_map/reduce_sum | solution.py:135
  792.2 2.7 pad_maximum_fusion.32
  794.8 37.0 %psum.7 = f32[4]{0:T(128)S(1)} all-reduce(f32[4]{0:T(128)S(1)} %pad_maximum_fusion.32), channel_id=1, replica_groups=mesh['gx'=8,'gy'=4] {'gx','gy'}, use_global_device_ids=true, to_apply=%region_4.0 | all-reduce | flops 4 | bytes 32 | tf_op jit(solution)/shard_map/psum | solution.py:137
  832.5 1.2 pad_maximum_fusion.33
  834.3 0.9 broadcast_divide_fusion
  (120 shorter events, 11.9 us)
Async XLA Ops:
  0.6 89.2 %copy-start.1 = (f32[256,512]{1,0:T(8,128)S(1)}, f32[256,512]{1,0:T(8,128)}, u32[]{:S(2)}) copy-start(f32[256,512]{1,0:T(8,128)} %param.6) | copy-start | bytes 1572868
  0.6 92.4 %copy-start.29 = (f32[4,8]{1,0:T(4,128)S(1)}, f32[4,8]{1,0:T(4,128)}, u32[]{:S(2)}) copy-start(f32[4,8]{1,0:T(4,128)} %param.11) | copy-start | bytes 388
  1.7 88.1 %collective-permute-start = (f32[66,512]{1,0:T(8,128)S(1)}, f32[66,512]{1,0:T(8,128)S(1)}, u32[]{:S(2)}, u32[]{:S(2)}) collective-permute-start(f32[66,512]{1,0:T(8,128)S(1)} %get-tuple-element.67), channel_id=1, source_target_pairs={{0,4},{4,8},{8,12},{12,16},{16,20},{20,24},{24,28},{28,0},{1,5},{5... | collective-permute-start | bytes 405512 | tf_op jit(solution)/shard_map/ppermute | solution.py:23
  2.3 87.6 %collective-permute-start.1 = (f32[66,512]{1,0:T(8,128)S(1)}, f32[66,512]{1,0:T(8,128)S(1)}, u32[]{:S(2)}, u32[]{:S(2)}) collective-permute-start(f32[66,512]{1,0:T(8,128)S(1)} %get-tuple-element.68), channel_id=1, source_target_pairs={{4,0},{8,4},{12,8},{16,12},{20,16},{24,20},{28,24},{0,28},{5,1},{9... | collective-permute-start | bytes 405512 | tf_op jit(solution)/shard_map/ppermute | solution.py:25
  90.0 8.6 %collective-permute-start.2 = (f32[388,66]{1,0:T(8,128)S(1)}, f32[388,66]{1,0:T(8,128)S(1)}, u32[]{:S(2)}, u32[]{:S(2)}) collective-permute-start(f32[388,66]{1,0:T(8,128)S(1)} %get-tuple-element.51), channel_id=1, source_target_pairs={{0,1},{1,2},{2,3},{3,0},{4,5},{5,6},{6,7},{7,4},{8,9},{9,10},{10,1... | collective-permute-start | bytes 307304 | tf_op jit(solution)/shard_map/ppermute | solution.py:23
  92.0 8.8 %collective-permute-start.3 = (f32[388,66]{1,0:T(8,128)S(1)}, f32[388,66]{1,0:T(8,128)S(1)}, u32[]{:S(2)}, u32[]{:S(2)}) collective-permute-start(f32[388,66]{1,0:T(8,128)S(1)} %get-tuple-element.52), channel_id=1, source_target_pairs={{1,0},{2,1},{3,2},{0,3},{5,4},{6,5},{7,6},{4,7},{9,8},{10,9},{11,1... | collective-permute-start | bytes 307304 | tf_op jit(solution)/shard_map/ppermute | solution.py:25
  101.2 75.0 %copy-start.28 = (s32[4,8,2]{1,2,0:T(2,128)S(1)}, s32[4,8,2]{1,2,0:T(2,128)}, u32[]{:S(2)}) copy-start(s32[4,8,2]{1,2,0:T(2,128)} %param.10) | copy-start | bytes 772
  131.5 84.5 %collective-permute-start.4 = (f32[66,512]{1,0:T(8,128)S(1)}, f32[66,512]{1,0:T(8,128)S(1)}, u32[]{:S(2)}, u32[]{:S(2)}) collective-permute-start(f32[66,512]{1,0:T(8,128)S(1)} %get-tuple-element.65), channel_id=1, source_target_pairs={{0,4},{4,8},{8,12},{12,16},{16,20},{20,24},{24,28},{28,0},{1,5},{5... | collective-permute-start | bytes 405512 | tf_op jit(solution)/shard_map/ppermute | solution.py:23
  131.6 84.4 %collective-permute-start.5 = (f32[66,512]{1,0:T(8,128)S(1)}, f32[66,512]{1,0:T(8,128)S(1)}, u32[]{:S(2)}, u32[]{:S(2)}) collective-permute-start(f32[66,512]{1,0:T(8,128)S(1)} %get-tuple-element.66), channel_id=1, source_target_pairs={{4,0},{8,4},{12,8},{16,12},{20,16},{24,20},{28,24},{0,28},{5,1},{9... | collective-permute-start | bytes 405512 | tf_op jit(solution)/shard_map/ppermute | solution.py:25
  216.1 8.1 collective-permute-start.6
  217.7 7.8 collective-permute-start.7
  225.9 34.8 %copy-start.2 = (f32[256,512]{1,0:T(8,128)S(1)}, f32[256,512]{1,0:T(8,128)}, u32[]{:S(2)}) copy-start(f32[256,512]{1,0:T(8,128)} %param.8) | copy-start | bytes 1572868
  257.2 59.9 %collective-permute-start.8 = (f32[66,512]{1,0:T(8,128)S(1)}, f32[66,512]{1,0:T(8,128)S(1)}, u32[]{:S(2)}, u32[]{:S(2)}) collective-permute-start(f32[66,512]{1,0:T(8,128)S(1)} %get-tuple-element.63), channel_id=1, source_target_pairs={{0,4},{4,8},{8,12},{12,16},{16,20},{20,24},{24,28},{28,0},{1,5},{5... | collective-permute-start | bytes 405512 | tf_op jit(solution)/shard_map/ppermute | solution.py:23
  257.2 59.9 %collective-permute-start.9 = (f32[66,512]{1,0:T(8,128)S(1)}, f32[66,512]{1,0:T(8,128)S(1)}, u32[]{:S(2)}, u32[]{:S(2)}) collective-permute-start(f32[66,512]{1,0:T(8,128)S(1)} %get-tuple-element.64), channel_id=1, source_target_pairs={{4,0},{8,4},{12,8},{16,12},{20,16},{24,20},{28,24},{0,28},{5,1},{9... | collective-permute-start | bytes 405512 | tf_op jit(solution)/shard_map/ppermute | solution.py:25
  261.5 217.7 %collective-permute-start.16 = (f32[66,512]{1,0:T(8,128)}, f32[66,512]{1,0:T(8,128)S(1)}, u32[]{:S(2)}, u32[]{:S(2)}) collective-permute-start(f32[66,512]{1,0:T(8,128)} %get-tuple-element.69), channel_id=1, source_target_pairs={{0,4},{4,8},{8,12},{12,16},{16,20},{20,24},{24,28},{28,0},{1,5},{5... | collective-permute-start | bytes 405512 | tf_op jit(solution)/shard_map/ppermute | solution.py:23
  261.5 217.7 %collective-permute-start.17 = (f32[66,512]{1,0:T(8,128)}, f32[66,512]{1,0:T(8,128)S(1)}, u32[]{:S(2)}, u32[]{:S(2)}) collective-permute-start(f32[66,512]{1,0:T(8,128)} %get-tuple-element.70), channel_id=1, source_target_pairs={{4,0},{8,4},{12,8},{16,12},{20,16},{24,20},{28,24},{0,28},{5,1},{9... | collective-permute-start | bytes 405512 | tf_op jit(solution)/shard_map/ppermute | solution.py:25
  317.2 126.9 %collective-permute-start.10 = (f32[388,66]{1,0:T(8,128)S(1)}, f32[388,66]{1,0:T(8,128)S(1)}, u32[]{:S(2)}, u32[]{:S(2)}) collective-permute-start(f32[388,66]{1,0:T(8,128)S(1)} %get-tuple-element.47), channel_id=1, source_target_pairs={{0,1},{1,2},{2,3},{3,0},{4,5},{5,6},{6,7},{7,4},{8,9},{9,10},{10,1... | collective-permute-start | bytes 307304 | tf_op jit(solution)/shard_map/ppermute | solution.py:23
  318.8 125.4 %collective-permute-start.11 = (f32[388,66]{1,0:T(8,128)S(1)}, f32[388,66]{1,0:T(8,128)S(1)}, u32[]{:S(2)}, u32[]{:S(2)}) collective-permute-start(f32[388,66]{1,0:T(8,128)S(1)} %get-tuple-element.48), channel_id=1, source_target_pairs={{1,0},{2,1},{3,2},{0,3},{5,4},{6,5},{7,6},{4,7},{9,8},{10,9},{11,1... | collective-permute-start | bytes 307304 | tf_op jit(solution)/shard_map/ppermute | solution.py:25
  475.6 6.7 collective-permute-start.12
  475.6 6.7 collective-permute-start.13
  479.3 8.8 %collective-permute-start.18 = (f32[388,66]{1,0:T(8,128)S(1)}, f32[388,66]{1,0:T(8,128)S(1)}, u32[]{:S(2)}, u32[]{:S(2)}) collective-permute-start(f32[388,66]{1,0:T(8,128)S(1)} %get-tuple-element.53), channel_id=1, source_target_pairs={{0,1},{1,2},{2,3},{3,0},{4,5},{5,6},{6,7},{7,4},{8,9},{9,10},{10,1... | collective-permute-start | bytes 307304 | tf_op jit(solution)/shard_map/ppermute | solution.py:23
  480.0 12.5 %collective-permute-start.19 = (f32[388,66]{1,0:T(8,128)S(1)}, f32[388,66]{1,0:T(8,128)S(1)}, u32[]{:S(2)}, u32[]{:S(2)}) collective-permute-start(f32[388,66]{1,0:T(8,128)S(1)} %get-tuple-element.54), channel_id=1, source_target_pairs={{1,0},{2,1},{3,2},{0,3},{5,4},{6,5},{7,6},{4,7},{9,8},{10,9},{11,1... | collective-permute-start | bytes 307304 | tf_op jit(solution)/shard_map/ppermute | solution.py:25
  482.3 12.7 %copy-start.26 = (f32[66,512]{1,0:T(8,128)}, f32[66,512]{1,0:T(8,128)S(1)}, u32[]{:S(2)}) copy-start(f32[66,512]{1,0:T(8,128)S(1)} %collective-permute-done.12) | copy-start | bytes 405508
  482.3 12.6 %copy-start.27 = (f32[66,512]{1,0:T(8,128)}, f32[66,512]{1,0:T(8,128)S(1)}, u32[]{:S(2)}) copy-start(f32[66,512]{1,0:T(8,128)S(1)} %collective-permute-done.13) | copy-start | bytes 405508
  482.4 12.5 %collective-permute-start.14 = (f32[388,66]{1,0:T(8,128)S(1)}, f32[388,66]{1,0:T(8,128)S(1)}, u32[]{:S(2)}, u32[]{:S(2)}) collective-permute-start(f32[388,66]{1,0:T(8,128)S(1)} %get-tuple-element.45), channel_id=1, source_target_pairs={{0,1},{1,2},{2,3},{3,0},{4,5},{5,6},{6,7},{7,4},{8,9},{9,10},{10,1... | collective-permute-start | bytes 307304 | tf_op jit(solution)/shard_map/ppermute | solution.py:23
  482.8 14.4 %collective-permute-start.15 = (f32[388,66]{1,0:T(8,128)S(1)}, f32[388,66]{1,0:T(8,128)S(1)}, u32[]{:S(2)}, u32[]{:S(2)}) collective-permute-start(f32[388,66]{1,0:T(8,128)S(1)} %get-tuple-element.46), channel_id=1, source_target_pairs={{1,0},{2,1},{3,2},{0,3},{5,4},{6,5},{7,6},{4,7},{9,8},{10,9},{11,1... | collective-permute-start | bytes 307304 | tf_op jit(solution)/shard_map/ppermute | solution.py:25
  644.2 6.4 collective-permute-start.20
  644.2 6.4 collective-permute-start.21
  650.6 16.2 %copy-start.25 = (f32[256,512]{1,0:T(8,128)S(1)}, f32[256,512]{1,0:T(8,128)}, u32[]{:S(2)}) copy-start(f32[256,512]{1,0:T(8,128)} %get-tuple-element.19) | copy-start | bytes 1572868
  651.4 13.9 %collective-permute-start.22 = (f32[388,66]{1,0:T(8,128)}, f32[388,66]{1,0:T(8,128)S(1)}, u32[]{:S(2)}, u32[]{:S(2)}) collective-permute-start(f32[388,66]{1,0:T(8,128)} %get-tuple-element.43), channel_id=1, source_target_pairs={{0,1},{1,2},{2,3},{3,0},{4,5},{5,6},{6,7},{7,4},{8,9},{9,10},{10,1... | collective-permute-start | bytes 307304 | tf_op jit(solution)/shard_map/ppermute | solution.py:23
  652.0 13.3 %collective-permute-start.23 = (f32[388,66]{1,0:T(8,128)S(1)}, f32[388,66]{1,0:T(8,128)}, u32[]{:S(2)}, u32[]{:S(2)}) collective-permute-start(f32[388,66]{1,0:T(8,128)S(1)} %get-tuple-element.44), channel_id=1, source_target_pairs={{1,0},{2,1},{3,2},{0,3},{5,4},{6,5},{7,6},{4,7},{9,8},{10,9},{11,1... | collective-permute-start | bytes 307304 | tf_op jit(solution)/shard_map/ppermute | solution.py:25
  656.9 9.9 %copy-start.24 = (f32[256,512]{1,0:T(8,128)S(1)}, f32[256,512]{1,0:T(8,128)}, u32[]{:S(2)}) copy-start(f32[256,512]{1,0:T(8,128)} %get-tuple-element.18) | copy-start | bytes 1572868
  693.0 7.9 collective-permute-start.24
  693.1 7.8 collective-permute-start.25
  700.9 16.2 %copy-start.15 = (f32[256,512]{1,0:T(8,128)S(1)}, f32[256,512]{1,0:T(8,128)}, u32[]{:S(2)}) copy-start(f32[256,512]{1,0:T(8,128)} %get-tuple-element.26) | copy-start | bytes 1572868
  700.9 16.2 %copy-start.16 = (f32[256,512]{1,0:T(8,128)S(1)}, f32[256,512]{1,0:T(8,128)}, u32[]{:S(2)}) copy-start(f32[256,512]{1,0:T(8,128)} %get-tuple-element.27) | copy-start | bytes 1572868
  700.9 16.2 %copy-start.17 = (f32[256,512]{1,0:T(8,128)S(1)}, f32[256,512]{1,0:T(8,128)}, u32[]{:S(2)}) copy-start(f32[256,512]{1,0:T(8,128)} %get-tuple-element.28) | copy-start | bytes 1572868
  700.9 16.2 %copy-start.18 = (f32[256,512]{1,0:T(8,128)S(1)}, f32[256,512]{1,0:T(8,128)}, u32[]{:S(2)}) copy-start(f32[256,512]{1,0:T(8,128)} %get-tuple-element.29) | copy-start | bytes 1572868
  701.8 13.7 %collective-permute-start.26 = (f32[388,66]{1,0:T(8,128)}, f32[388,66]{1,0:T(8,128)}, u32[]{:S(2)}, u32[]{:S(2)}) collective-permute-start(f32[388,66]{1,0:T(8,128)} %get-tuple-element.41), channel_id=1, source_target_pairs={{0,1},{1,2},{2,3},{3,0},{4,5},{5,6},{6,7},{7,4},{8,9},{9,10},{10,1... | collective-permute-start | bytes 307304 | tf_op jit(solution)/shard_map/ppermute | solution.py:23
  701.8 13.7 %collective-permute-start.27 = (f32[388,66]{1,0:T(8,128)}, f32[388,66]{1,0:T(8,128)}, u32[]{:S(2)}, u32[]{:S(2)}) collective-permute-start(f32[388,66]{1,0:T(8,128)} %get-tuple-element.42), channel_id=1, source_target_pairs={{1,0},{2,1},{3,2},{0,3},{5,4},{6,5},{7,6},{4,7},{9,8},{10,9},{11,1... | collective-permute-start | bytes 307304 | tf_op jit(solution)/shard_map/ppermute | solution.py:25
  743.3 6.7 collective-permute-start.28
  743.4 6.6 collective-permute-start.29
  750.0 16.2 %copy-start.7 = (f32[256,512]{1,0:T(8,128)S(1)}, f32[256,512]{1,0:T(8,128)}, u32[]{:S(2)}) copy-start(f32[256,512]{1,0:T(8,128)} %get-tuple-element.35) | copy-start | bytes 1572868
  750.0 16.2 %copy-start.8 = (f32[256,512]{1,0:T(8,128)S(1)}, f32[256,512]{1,0:T(8,128)}, u32[]{:S(2)}) copy-start(f32[256,512]{1,0:T(8,128)} %get-tuple-element.36) | copy-start | bytes 1572868
  750.0 16.2 %copy-start.9 = (f32[256,512]{1,0:T(8,128)S(1)}, f32[256,512]{1,0:T(8,128)}, u32[]{:S(2)}) copy-start(f32[256,512]{1,0:T(8,128)} %get-tuple-element.37) | copy-start | bytes 1572868
  750.0 16.2 %copy-start.10 = (f32[256,512]{1,0:T(8,128)S(1)}, f32[256,512]{1,0:T(8,128)}, u32[]{:S(2)}) copy-start(f32[256,512]{1,0:T(8,128)} %get-tuple-element.38) | copy-start | bytes 1572868
  750.8 13.7 %collective-permute-start.30 = (f32[388,66]{1,0:T(8,128)}, f32[388,66]{1,0:T(8,128)}, u32[]{:S(2)}, u32[]{:S(2)}) collective-permute-start(f32[388,66]{1,0:T(8,128)} %get-tuple-element.39), channel_id=1, source_target_pairs={{0,1},{1,2},{2,3},{3,0},{4,5},{5,6},{6,7},{7,4},{8,9},{9,10},{10,1... | collective-permute-start | bytes 307304 | tf_op jit(solution)/shard_map/ppermute | solution.py:23
  750.9 13.7 %collective-permute-start.31 = (f32[388,66]{1,0:T(8,128)}, f32[388,66]{1,0:T(8,128)}, u32[]{:S(2)}, u32[]{:S(2)}) collective-permute-start(f32[388,66]{1,0:T(8,128)} %get-tuple-element.40), channel_id=1, source_target_pairs={{1,0},{2,1},{3,2},{0,3},{5,4},{6,5},{7,6},{4,7},{9,8},{10,9},{11,1... | collective-permute-start | bytes 307304 | tf_op jit(solution)/shard_map/ppermute | solution.py:25
  (14 other events, 29.6 us)
where the time goes:
time: 849 us; the launch traced here: 836 us
  between operations  369 us (43%)
  other arithmetic  332 us (39%)
  starting transfers between devices  54.5 us (6%)
  blocking collectives  37 us (4%)
  waiting for transfers between devices  33.9 us (4%)
  local copies, waits for them, and re-layouts  8.8 us (1%)
    reduce_sum x4, other arithmetic, shards(): local_sums.append(jnp.sum(arrived))  224 us
    min x3, other arithmetic, policy(): lowest = reduce(jnp.minimum, candidates)  92.4 us
    ppermute x16, starting transfers between devices, with_halo(): lax.ppermute(head, axis, [((i + 1) % count, i) for i in range(count)])  47 us
    psum x1, blocking collectives, shards(): totals = lax.psum(jnp.stack(local_sums), ('gx', 'gy')) / cells  37 us
    ppermute x16, waiting for transfers between devices, with_halo(): lax.ppermute(tail, axis, [(i, (i + 1) % count) for i in range(count)])  23.9 us
  transfers between devices with their start and end apart: 32, of which 11 were waited for; matrix products, arithmetic and copies ran while one was open for 5% of the time, Pallas kernels for 0%

commit v1 on v0

v1 whole, which is shorter than its diff:
```python
import functools

import jax
import jax.numpy as jnp
from jax import lax
from jax.experimental import pallas as pl
from jax.experimental.pallas import tpu as pltpu
from jax.sharding import PartitionSpec as P

REACH = 64
LANES = 128
SUBLANES = 8
TAPS = 4
FIELDS = 3 * TAPS
ROW_HALO = -(-(REACH + 2) // SUBLANES) * SUBLANES

time_step = 0.1
temper = 0.3
epsilon = 1e-06


def catmull(fraction):
    square = fraction * fraction
    cube = square * fraction
    return [
        (-cube + 2.0 * square - fraction) * 0.5,
        (3.0 * cube - 5.0 * square + 2.0) * 0.5,
        (-3.0 * cube + 4.0 * square + fraction) * 0.5,
        (cube - square) * 0.5,
    ]


def shift_table(offsets, padded_rows):
    taps = jnp.arange(TAPS, dtype=jnp.int32) - 1
    tables = []
    for sign in (1, -1):
        move = sign * offsets[..., 1:] + taps
        around = jnp.where(move < 0, move + LANES, move)
        row = ROW_HALO - 1 + sign * offsets[..., :1] + jnp.where(move < 0, 0, padded_rows)
        tables.append(jnp.concatenate([row, (LANES - around) % LANES, LANES - around], axis=-1))
    return jnp.stack(tables).astype(jnp.int32).reshape(-1)


def stage(tiles, top, bottom, left, right, padded):
    height = tiles[0].shape[0]
    count = len(tiles)
    pitch = padded.shape[0] // (count + 2)
    for tile in range(count):
        at = (tile + 1) * pitch
        padded[at : at + ROW_HALO, :] = top[tile]
        padded[at + ROW_HALO : at + ROW_HALO + height, :] = tiles[tile][...]
        padded[at + ROW_HALO + height : at + 2 * ROW_HALO + height, :] = bottom[tile]
    if left is not None:
        at = (count + 1) * pitch
        padded[0 : 2 * ROW_HALO + height, :] = left[...]
        padded[at : at + 2 * ROW_HALO + height, :] = right[...]


def shift_block(table, entry, pairs, wanted, block, pitch, padded, cuts, shifted):
    start = pl.multiple_of(block * SUBLANES, SUBLANES)
    for k, tap in pairs:
        at = entry + k * FIELDS + tap
        row = table[at] + start
        turn = table[at + TAPS]
        keep = cuts[k * TAPS + tap] > 0
        turned = {}
        for tile in wanted:
            for part in (tile, tile + 1):
                if part not in turned:
                    turned[part] = pltpu.roll(padded[pl.ds(row + part * pitch, SUBLANES), :], turn, 1)
        for n, tile in enumerate(wanted):
            shifted[k, n, tap, pl.ds(start, SUBLANES), :] = jnp.where(keep, turned[tile], turned[tile + 1])


def interpolate(shifted, k, n, start, weights):
    summed = None
    for row_tap in range(TAPS):
        partial_sum = None
        for col_tap in range(TAPS):
            piece = shifted[k, n, col_tap, pl.ds(start + row_tap, SUBLANES), :]
            term = weights[row_tap][col_tap] * piece
            partial_sum = term if partial_sum is None else partial_sum + term
        summed = partial_sum if summed is None else summed + partial_sum
    return summed


def products(fraction, here):
    weights_x = catmull(fraction[0, 0, here, :])
    weights_y = catmull(fraction[0, 1, here, :])
    return [[x * y for y in weights_y] for x in weights_x]


def sweep(table, entry, wanted, rows, pitch, padded, cuts, shifted, finish, carry):
    controls = shifted.shape[0]
    chunk = pl.program_id(0)
    first = chunk * (rows // SUBLANES)
    blocks = shifted.shape[3] // SUBLANES
    pairs = [(k, tap) for k in range(controls) for tap in range(TAPS)]

    @pl.when(chunk == 0)
    def _():
        lane = lax.broadcasted_iota(jnp.int32, (SUBLANES, LANES), 1)
        for k, tap in pairs:
            cuts[k * TAPS + tap] = table[entry + k * FIELDS + 2 * TAPS + tap] - lane

        def ahead(block, nothing):
            shift_block(table, entry, pairs, wanted, block, pitch, padded, cuts, shifted)
            return nothing

        lax.fori_loop(0, blocks, ahead, 0, unroll=3 if blocks % 3 == 0 else 1)

    def one_block(block, carry):
        start = pl.multiple_of((first + block) * SUBLANES, SUBLANES)
        here = pl.ds(pl.multiple_of(block * SUBLANES, SUBLANES), SUBLANES)
        for n in range(len(wanted)):

            def sampled(k, weights):
                return interpolate(shifted, k, n, start, weights)

            carry = finish(n, start, here, sampled, carry)
        return carry

    return lax.fori_loop(0, rows // SUBLANES, one_block, carry)


def edges_out(values, inner_top, inner_bottom, top, bottom):
    height = values[0].shape[0]
    if inner_top is None:
        for n in range(len(values)):
            top[n] = values[n][0:ROW_HALO, :]
            bottom[n] = values[n][height - ROW_HALO : height, :]
        return
    count = top.shape[0]
    for n, tile in enumerate((0, count - 1)):
        top[tile] = values[n][0:ROW_HALO, :]
        bottom[tile] = values[n][height - ROW_HALO : height, :]
    for tile in range(1, count - 1):
        top[tile] = inner_top[tile - 1]
        bottom[tile] = inner_bottom[tile - 1]


def step_kernel(wanted, count, moment_entry, cost_entry, rows, is_backward, is_outer, *refs):
    refs = list(refs)
    take = lambda n: [refs.pop(0) for _ in range(n)]
    (table,) = take(1)
    costs = take(1)[0] if is_backward else None
    tiles = take(count)
    top, bottom = take(2)
    left, right, inner_top, inner_bottom = take(4) if is_outer else (None,) * 4
    fractions = take(len(wanted))
    if is_backward:
        crowding = take(len(wanted))
    else:
        ramps, inverse = take(2)
    values = take(len(wanted))
    edge_top, edge_bottom = take(2)
    if is_backward:
        ramps, inverse = take(2)
    else:
        (mass,) = take(1)
    padded, cuts, shifted = take(3)
    pitch = padded.shape[0] // (count + 2)
    controls = shifted.shape[0]

    @pl.when(pl.program_id(0) == 0)
    def _():
        stage(tiles, top, bottom, left, right, padded)
        if not is_backward:
            mass[...] = jnp.zeros_like(mass)

    def finish_backward(n, start, here, sampled, carry):
        weights = products(fractions[n], here)
        candidates = [sampled(k, weights) + costs[cost_entry + k] for k in range(controls)]
        lowest = functools.reduce(jnp.minimum, candidates)
        values[n][pl.ds(start, SUBLANES), :] = lowest + time_step * crowding[n][here, :]
        level = lowest + temper
        total = None
        for k in range(controls):
            ramp = jnp.maximum(level - candidates[k], 0.0)
            ramps[n, k, here, :] = ramp
            total = ramp if total is None else total + ramp
        inverse[n, here, :] = 1.0 / total
        return carry

    def finish_forward(n, start, here, sampled, sums):
        weights = products(fractions[n], here)
        total = None
        for k in range(controls):
            term = ramps[n, k, here, :] * sampled(k, weights)
            total = term if total is None else total + term
        total = jnp.maximum(total * inverse[n, here, :], 0.0)
        values[n][pl.ds(start, SUBLANES), :] = total
        return sums + total

    if is_backward:
        sweep(table, moment_entry, wanted, rows, pitch, padded, cuts, shifted, finish_backward, 0)
    else:
        zero = jnp.zeros((SUBLANES, LANES), jnp.float32)
        mass[...] += sweep(table, moment_entry, wanted, rows, pitch, padded, cuts, shifted, finish_forward, zero)

    @pl.when(pl.program_id(0) == pl.num_programs(0) - 1)
    def _():
        edges_out(values, inner_top, inner_bottom, edge_top, edge_bottom)


def padded_rows(height):
    return height + 2 * ROW_HALO + SUBLANES


def row_chunk(height):
    for rows in (64, 32, 16, 8):
        if height % rows == 0:
            return rows
    return height


def step(wanted, entry, cost_entry, controls, moment, table, tiles, halo, sides, inner, fractions, backward, forward):
    is_backward, is_outer = backward is not None, sides is not None
    height = tiles[0].shape[0]
    count = len(tiles)
    group = len(wanted)
    rows = row_chunk(height)
    whole = lambda *shape: pl.BlockSpec(shape, lambda c: (0,) * len(shape))
    smem = pl.BlockSpec(memory_space=pltpu.SMEM)
    edge = whole(count, ROW_HALO, LANES)
    inner_edge = whole(count - 2, ROW_HALO, LANES)
    fraction = [
        pl.BlockSpec((1, 2, rows, LANES), functools.partial(lambda t, c: (moment, 0, c, t), tile)) for tile in wanted
    ]
    ramp = pl.BlockSpec((group, controls, rows, LANES), lambda c: (0, 0, c, 0))
    inverse = pl.BlockSpec((group, rows, LANES), lambda c: (0, c, 0))
    f32 = lambda *shape: jax.ShapeDtypeStruct(shape, jnp.float32)

    args, specs = [table], [smem]
    if is_backward:
        args, specs = args + [backward[0]], specs + [smem]
    args += [*tiles, *halo]
    specs += [whole(height, LANES)] * count + [edge] * 2
    if is_outer:
        args += [*sides, *inner]
        specs += [whole(height + 2 * ROW_HALO, LANES)] * 2 + [inner_edge] * 2
    args += [fractions] * group
    specs += fraction
    if is_backward:
        args += [backward[1]] * group
        specs += [pl.BlockSpec((rows, LANES), functools.partial(lambda t, c: (c, t), tile)) for tile in wanted]
    else:
        args += [*forward]
        specs += [ramp, inverse]

    edge_count = count if is_outer else group
    outs = [f32(height, LANES)] * group + [f32(edge_count, ROW_HALO, LANES)] * 2
    out_specs = [whole(height, LANES)] * group + [whole(edge_count, ROW_HALO, LANES)] * 2
    if is_backward:
        outs += [f32(group, controls, height, LANES), f32(group, height, LANES)]
        out_specs += [ramp, inverse]
    else:
        outs += [f32(SUBLANES, LANES)]
        out_specs += [whole(SUBLANES, LANES)]
    results = pl.pallas_call(
        functools.partial(step_kernel, wanted, count, entry, cost_entry, rows, is_backward, is_outer),
        grid=(height // rows,),
        in_specs=specs,
        out_specs=out_specs,
        out_shape=outs,
        scratch_shapes=[
            pltpu.VMEM(((count + 2) * padded_rows(height), LANES), jnp.float32),
            pltpu.VMEM((controls * TAPS, SUBLANES, LANES), jnp.int32),
            pltpu.VMEM((controls, group, TAPS, height + SUBLANES, LANES), jnp.float32),
        ],
        cost_estimate=pl.CostEstimate(
            flops=64 * controls * group * height * LANES,
            bytes_accessed=4 * (controls + 6) * group * height * LANES,
            transcendentals=0,
        ),
        name=("backward" if is_backward else "forward") + ("_outer" if is_outer else "_inner"),
    )(*args)
    return results[:group], results[group : group + 2], results[group + 2 :]


def split_kernel(cells, *outs):
    *tiles, top, bottom = outs
    height = cells.shape[0]
    for n, tile in enumerate(tiles):
        piece = cells[:, n * LANES : (n + 1) * LANES]
        tile[...] = piece
        top[n] = piece[0:ROW_HALO, :]
        bottom[n] = piece[height - ROW_HALO : height, :]


def split(cells):
    height, breadth = cells.shape
    count = breadth // LANES
    f32 = lambda *shape: jax.ShapeDtypeStruct(shape, jnp.float32)
    results = pl.pallas_call(
        split_kernel,
        out_shape=[f32(height, LANES)] * count + [f32(count, ROW_HALO, LANES)] * 2,
        name="split",
    )(cells)
    return results[:count], results[count:]


def columns_kernel(top, bottom, first, last, first_out, last_out):
    height = first.shape[0]
    for tile, cells, out in ((0, first, first_out), (top.shape[0] - 1, last, last_out)):
        out[0:ROW_HALO, :] = top[tile]
        out[ROW_HALO : ROW_HALO + height, :] = cells[...]
        out[ROW_HALO + height : 2 * ROW_HALO + height, :] = bottom[tile]


def columns(halo, first, last):
    out = jax.ShapeDtypeStruct((first.shape[0] + 2 * ROW_HALO, LANES), jnp.float32)
    return pl.pallas_call(columns_kernel, out_shape=[out, out], name="columns")(*halo, first, last)


def passed(cells, axis, distance):
    count = lax.axis_size(axis)
    return lax.ppermute(cells, axis, [(i, (i + distance) % count) for i in range(count)])


def row_halo(edges):
    return passed(edges[1], "gx", 1), passed(edges[0], "gx", -1)


def column_halo(halo, tiles):
    first, last = columns(halo, tiles[0], tiles[-1])
    return passed(last, "gy", 1), passed(first, "gy", -1)


def everywhere(sums):
    for axis in ("gy", "gx"):
        count = lax.axis_size(axis)
        if count & (count - 1):
            sums = lax.psum(sums, axis)
            continue
        distance = 1
        while distance < count:
            sums = sums + lax.ppermute(sums, axis, [(i, i ^ distance) for i in range(count)])
            distance *= 2
    return sums


def shards(terminal, crowding, density, fractions, offsets, control_cost):
    height, breadth = terminal.shape
    count = breadth // LANES
    steps_count, controls = control_cost.shape
    cells = height * breadth * lax.axis_size("gx") * lax.axis_size("gy")
    table = shift_table(offsets, padded_rows(height))
    costs = time_step * control_cost.reshape(-1)
    inside, outside = tuple(range(1, count - 1)), (0, count - 1)

    def both_groups(tiles, halo, entry, moment, backward, policy):
        sides = column_halo(halo, tiles)
        common = (entry, moment * controls, controls, moment, table, tiles, halo)
        inner, inner_edges, inner_rest = step(
            inside, *common, None, None, fractions, backward, None if policy is None else policy[0]
        )
        outer, edges, outer_rest = step(
            outside, *common, sides, inner_edges, fractions, backward, None if policy is None else policy[1]
        )
        return [outer[0], *inner, outer[1]], edges, (inner_rest, outer_rest)

    tiles, edges = split(terminal)
    policies = [None] * steps_count
    for moment in reversed(range(steps_count)):
        entry = moment * controls * FIELDS
        tiles, edges, policies[moment] = both_groups(
            tiles, row_halo(edges), entry, moment, (costs, crowding), None
        )
    value = jnp.concatenate(tiles, axis=1)

    tiles, edges = split(density)
    local_sums = []
    for moment in range(steps_count):
        entry = (steps_count + moment) * controls * FIELDS
        tiles, edges, ((inner_mass,), (outer_mass,)) = both_groups(
            tiles, row_halo(edges), entry, moment, None, policies[moment]
        )
        local_sums.append(jnp.sum(inner_mass + outer_mass))
    totals = everywhere(jnp.stack(local_sums)) / cells
    masses = []
    scale = jnp.float32(1.0)
    for moment in range(steps_count):
        masses.append(totals[moment] / scale)
        scale = totals[moment] + epsilon * scale
    return (value, jnp.concatenate(tiles, axis=1) / scale, jnp.stack(masses))


def solution(mesh):
    return jax.shard_map(
        shards,
        mesh=mesh,
        in_specs=(P("gx", "gy"), P("gx", "gy"), P("gx", "gy"), P(None, None, "gx", "gy"), P(), P()),
        out_specs=(P("gx", "gy"), P("gx", "gy"), P()),
        check_vma=False,
    )
```

time: 849 us -> 320 us (0.38); the launches traced: 836 us -> 317 us
  between operations: 369 us -> 5.57 us
  other arithmetic: 332 us -> 16.9 us
  Pallas kernels: 0 us -> 193 us
  blocking collectives: 37 us -> 0 us
    reduce_sum x4, other arithmetic: 224 us -> 3.76 us  [shards(): local_sums.append(jnp.sum(inner_mass + outer_mass))]
    pallas_call x0 -> x26, Pallas kernels: none -> 193 us  [the longest x16 174 us: step(): pl.pallas_call(functools.partial(step_kernel, wanted, count, entry, cost_...]
    min x3 -> x0, other arithmetic: 92.4 us -> none  [policy(): lowest = reduce(jnp.minimum, candidates)]
    psum x1 -> x0, blocking collectives: 37 us -> none  [shards(): totals = lax.psum(jnp.stack(local_sums), ('gx', 'gy')) / cells]
    unnamed x60 -> x88, local copies, waits for them, and re-layouts: 0.15 us -> 11.6 us
    ppermute x32 -> x37, waiting for transfers between devices: 33.9 us -> 32.3 us  [the longest x32 18.5 us: passed(): lax.ppermute(cells, axis, [(i, (i + distance) % count) for i in range(cou...]
    ppermute x32 -> x37, starting transfers between devices: 54.5 us -> 55.6 us  [the longest x32 53 us: passed(): lax.ppermute(cells, axis, [(i, (i + distance) % count) for i in range(cou...]
  transfers between devices with their start and end apart: 32 -> 37, of which waited for: 11 -> 11; matrix products, arithmetic and copies ran while one was open for 5% -> 2% of each run, Pallas kernels for 0% -> 31%
where the time goes in v1:
time: 320 us; the launch traced here: 317 us
  Pallas kernels  193 us (60%)
  starting transfers between devices  55.6 us (17%)
  waiting for transfers between devices  32.3 us (10%)
  other arithmetic  16.9 us (5%)
  local copies, waits for them, and re-layouts  13.6 us (4%)
  between operations  5.57 us (2%)
    pallas_call x16, Pallas kernels, step(): pl.pallas_call(functools.partial(step_kernel, wanted, count, entry, cost_...  174 us
    ppermute x32, starting transfers between devices, passed(): lax.ppermute(cells, axis, [(i, (i + distance) % count) for i in range(cou...  53 us
    ppermute x32, waiting for transfers between devices, passed(): lax.ppermute(cells, axis, [(i, (i + distance) % count) for i in range(cou...  18.5 us
    pallas_call x8, Pallas kernels, columns(): pl.pallas_call(columns_kernel, out_shape=[out, out], name='columns')  15.1 us
    ppermute x5, waiting for transfers between devices, everywhere(): lax.ppermute(sums, axis, [(i, i ^ distance) for i in range(count)])  13.8 us
    unnamed x88, local copies, waits for them, and re-layouts  11.6 us
  transfers between devices with their start and end apart: 37, of which 11 were waited for; matrix products, arithmetic and copies ran while one was open for 2% of the time, Pallas kernels for 31%

profile of v1, /device:TPU:0, one launch (start us, length us, event | category | flops | bytes accessed | tf_op | source)
XLA Modules:
  0.0 317.1 jit_solution(14799230729684270342)
XLA Ops:
  0.6 1.9 split.2
  3.1 4.0 %collective-permute-start.1 = (f32[4,72,128]{2,1,0:T(8,128)}, f32[4,72,128]{2,1,0:T(8,128)S(1)}, u32[]{:S(2)}, u32[]{:S(2)}) collective-permute-start(f32[4,72,128]{2,1,0:T(8,128)} %get-tuple-element.120), channel_id=1, source_target_pairs={{0,28},{4,0},{8,4},{12,8},{16,12},{20,16},{24,20},{28,24},{1,29},{... | collective-permute-start | bytes 442376 | tf_op jit(solution)/shard_map/ppermute | solution.py:318
  12.8 2.0 collective-permute-start.2
  17.1 10.4 %backward_inner.4 = (f32[256,128]{1,0:T(8,128)}, f32[256,128]{1,0:T(8,128)}, f32[2,72,128]{2,1,0:T(8,128)}, f32[2,72,128]{2,1,0:T(8,128)}, f32[2,8,256,128]{3,2,1,0:T(8,128)}, /*index=5*/f32[2,256,128]{2,1,0:T(8,128)}) custom-call(s32[768]{0:T(1024)} %reshape.19.refs_0_, f32[32]{0:T(128)} %mul.27.refs_1_, f32[256,128]{1,0:T(8,128)} %get-tuple-element.115.first.refs_2_, ...), custom_call_target="tpu_custom_call" | custom-call | flops 33554432 | bytes 3670016 | tf_op jit(solution)/shard_map/backward_inner/pallas_call | solution.py:260
  28.2 11.8 %backward_outer.4 = (f32[256,128]{1,0:T(8,128)}, f32[256,128]{1,0:T(8,128)}, f32[4,72,128]{2,1,0:T(8,128)}, f32[4,72,128]{2,1,0:T(8,128)}, f32[2,8,256,128]{3,2,1,0:T(8,128)}, /*index=5*/f32[2,256,128]{2,1,0:T(8,128)}) custom-call(s32[768]{0:T(1024)} %reshape.19.refs_0_, f32[32]{0:T(128)} %mul.27.refs_1_, f32[256,128]{1,0:T(8,128)} %get-tuple-element.115.first.refs_2_, ...), custom_call_target="tpu_custom_call" | custom-call | flops 33554432 | bytes 3670016 | tf_op jit(solution)/shard_map/backward_outer/pallas_call | solution.py:260
  41.0 2.6 collective-permute-start.5
  43.6 3.9 %collective-permute-done.4.top.refs_6_ = f32[4,72,128]{2,1,0:T(8,128)S(1)} collective-permute-done((f32[4,72,128]{2,1,0:T(8,128)}, f32[4,72,128]{2,1,0:T(8,128)S(1)}, u32[]{:S(2)}, u32[]{:S(2)}) %collective-permute-start.4) | collective-permute-done | bytes 147488 | tf_op jit(solution)/shard_map/ppermute | solution.py:318
  48.3 1.9 columns.9
  53.1 10.4 %backward_inner.5 = (f32[256,128]{1,0:T(8,128)}, f32[256,128]{1,0:T(8,128)}, f32[2,72,128]{2,1,0:T(8,128)}, f32[2,72,128]{2,1,0:T(8,128)}, f32[2,8,256,128]{3,2,1,0:T(8,128)}, /*index=5*/f32[2,256,128]{2,1,0:T(8,128)}) custom-call(s32[768]{0:T(1024)} %reshape.19.refs_0_, f32[32]{0:T(128)} %mul.27.refs_1_, f32[256,128]{1,0:T(8,128)} %get-tuple-element.125.first.refs_2_, ...), custom_call_target="tpu_custom_call" | custom-call | flops 33554432 | bytes 3670016 | tf_op jit(solution)/shard_map/backward_inner/pallas_call | solution.py:260
  64.3 11.8 %backward_outer.5 = (f32[256,128]{1,0:T(8,128)}, f32[256,128]{1,0:T(8,128)}, f32[4,72,128]{2,1,0:T(8,128)}, f32[4,72,128]{2,1,0:T(8,128)}, f32[2,8,256,128]{3,2,1,0:T(8,128)}, /*index=5*/f32[2,256,128]{2,1,0:T(8,128)}) custom-call(s32[768]{0:T(1024)} %reshape.19.refs_0_, f32[32]{0:T(128)} %mul.27.refs_1_, f32[256,128]{1,0:T(8,128)} %get-tuple-element.125.first.refs_2_, ...), custom_call_target="tpu_custom_call" | custom-call | flops 33554432 | bytes 3670016 | tf_op jit(solution)/shard_map/backward_outer/pallas_call | solution.py:260
  76.1 3.5 %collective-permute-start.9 = (f32[4,72,128]{2,1,0:T(8,128)}, f32[4,72,128]{2,1,0:T(8,128)S(1)}, u32[]{:S(2)}, u32[]{:S(2)}) collective-permute-start(f32[4,72,128]{2,1,0:T(8,128)} %get-tuple-element.140), channel_id=1, source_target_pairs={{0,28},{4,0},{8,4},{12,8},{16,12},{20,16},{24,20},{28,24},{1,29},{... | collective-permute-start | bytes 442376 | tf_op jit(solution)/shard_map/ppermute | solution.py:318
  79.6 3.8 %collective-permute-done.8.top.refs_6_ = f32[4,72,128]{2,1,0:T(8,128)S(1)} collective-permute-done((f32[4,72,128]{2,1,0:T(8,128)}, f32[4,72,128]{2,1,0:T(8,128)S(1)}, u32[]{:S(2)}, u32[]{:S(2)}) %collective-permute-start.8) | collective-permute-done | bytes 147488 | tf_op jit(solution)/shard_map/ppermute | solution.py:318
  84.1 1.9 columns.10
  86.8 2.1 collective-permute-start.11
  88.9 10.4 %backward_inner.6 = (f32[256,128]{1,0:T(8,128)}, f32[256,128]{1,0:T(8,128)}, f32[2,72,128]{2,1,0:T(8,128)}, f32[2,72,128]{2,1,0:T(8,128)}, f32[2,8,256,128]{3,2,1,0:T(8,128)}, /*index=5*/f32[2,256,128]{2,1,0:T(8,128)}) custom-call(s32[768]{0:T(1024)} %reshape.19.refs_0_, f32[32]{0:T(128)} %mul.27.refs_1_, f32[256,128]{1,0:T(8,128)} %get-tuple-element.135.first.refs_2_, ...), custom_call_target="tpu_custom_call" | custom-call | flops 33554432 | bytes 3670016 | tf_op jit(solution)/shard_map/backward_inner/pallas_call | solution.py:260
  100.1 11.8 %backward_outer.6 = (f32[256,128]{1,0:T(8,128)}, f32[256,128]{1,0:T(8,128)}, f32[4,72,128]{2,1,0:T(8,128)}, f32[4,72,128]{2,1,0:T(8,128)}, f32[2,8,256,128]{3,2,1,0:T(8,128)}, /*index=5*/f32[2,256,128]{2,1,0:T(8,128)}) custom-call(s32[768]{0:T(1024)} %reshape.19.refs_0_, f32[32]{0:T(128)} %mul.27.refs_1_, f32[256,128]{1,0:T(8,128)} %get-tuple-element.135.first.refs_2_, ...), custom_call_target="tpu_custom_call" | custom-call | flops 33554432 | bytes 3670016 | tf_op jit(solution)/shard_map/backward_outer/pallas_call | solution.py:260
  112.0 3.5 %collective-permute-start.13 = (f32[4,72,128]{2,1,0:T(8,128)}, f32[4,72,128]{2,1,0:T(8,128)S(1)}, u32[]{:S(2)}, u32[]{:S(2)}) collective-permute-start(f32[4,72,128]{2,1,0:T(8,128)} %get-tuple-element.150), channel_id=1, source_target_pairs={{0,28},{4,0},{8,4},{12,8},{16,12},{20,16},{24,20},{28,24},{1,29},{... | collective-permute-start | bytes 442376 | tf_op jit(solution)/shard_map/ppermute | solution.py:318
  115.5 2.0 split.3
  117.5 3.5 %collective-permute-start.17 = (f32[4,72,128]{2,1,0:T(8,128)}, f32[4,72,128]{2,1,0:T(8,128)S(1)}, u32[]{:S(2)}, u32[]{:S(2)}) collective-permute-start(f32[4,72,128]{2,1,0:T(8,128)} %get-tuple-element.164), channel_id=1, source_target_pairs={{0,28},{4,0},{8,4},{12,8},{16,12},{20,16},{24,20},{28,24},{1,29},{... | collective-permute-start | bytes 442376 | tf_op jit(solution)/shard_map/ppermute | solution.py:318
  121.7 1.9 columns.11
  124.1 2.4 collective-permute-start.15
  129.7 2.4 collective-permute-start.19
  132.0 10.5 %backward_inner.7 = (f32[256,128]{1,0:T(8,128)}, f32[256,128]{1,0:T(8,128)}, f32[2,72,128]{2,1,0:T(8,128)}, f32[2,72,128]{2,1,0:T(8,128)}, f32[2,8,256,128]{3,2,1,0:T(8,128)}, /*index=5*/f32[2,256,128]{2,1,0:T(8,128)}) custom-call(s32[768]{0:T(1024)} %reshape.19.refs_0_, f32[32]{0:T(128)} %mul.27.refs_1_, f32[256,128]{1,0:T(8,128)} %get-tuple-element.145.first.refs_2_, ...), custom_call_target="tpu_custom_call" | custom-call | flops 33554432 | bytes 3670016 | tf_op jit(solution)/shard_map/backward_inner/pallas_call | solution.py:260
  142.5 10.1 %forward_inner.4 = (f32[256,128]{1,0:T(8,128)}, f32[256,128]{1,0:T(8,128)}, f32[2,72,128]{2,1,0:T(8,128)}, f32[2,72,128]{2,1,0:T(8,128)}, f32[8,128]{1,0:T(8,128)}) custom-call(s32[768]{0:T(1024)} %reshape.19.refs_0_, f32[256,128]{1,0:T(8,128)} %get-tuple-element.159.first.refs_1_, f32[256,128]{1,0:T(8,128)} %get-tuple-element.160.refs_2_, ...), custom_call_target="tpu_custom_call" | custom-call | flops 33554432 | bytes 3670016 | tf_op jit(solution)/shard_map/forward_inner/pallas_call | solution.py:260
  153.4 11.8 %backward_outer.7 = (f32[256,128]{1,0:T(8,128)}, f32[256,128]{1,0:T(8,128)}, f32[4,72,128]{2,1,0:T(8,128)}, f32[4,72,128]{2,1,0:T(8,128)}, f32[2,8,256,128]{3,2,1,0:T(8,128)}, /*index=5*/f32[2,256,128]{2,1,0:T(8,128)}) custom-call(s32[768]{0:T(1024)} %reshape.19.refs_0_, f32[32]{0:T(128)} %mul.27.refs_1_, f32[256,128]{1,0:T(8,128)} %get-tuple-element.145.first.refs_2_, ...), custom_call_target="tpu_custom_call" | custom-call | flops 33554432 | bytes 3670016 | tf_op jit(solution)/shard_map/backward_outer/pallas_call | solution.py:260
  165.9 11.3 %forward_outer.4 = (f32[256,128]{1,0:T(8,128)}, f32[256,128]{1,0:T(8,128)}, f32[4,72,128]{2,1,0:T(8,128)}, f32[4,72,128]{2,1,0:T(8,128)}, f32[8,128]{1,0:T(8,128)}) custom-call(s32[768]{0:T(1024)} %reshape.19.refs_0_, f32[256,128]{1,0:T(8,128)} %get-tuple-element.159.first.refs_1_, f32[256,128]{1,0:T(8,128)} %get-tuple-element.160.refs_2_, ...), custom_call_target="tpu_custom_call" | custom-call | flops 33554432 | bytes 3670016 | tf_op jit(solution)/shard_map/forward_outer/pallas_call | solution.py:260
  177.2 3.5 %collective-permute-start.21 = (f32[4,72,128]{2,1,0:T(8,128)}, f32[4,72,128]{2,1,0:T(8,128)S(1)}, u32[]{:S(2)}, u32[]{:S(2)}) collective-permute-start(f32[4,72,128]{2,1,0:T(8,128)} %get-tuple-element.178), channel_id=1, source_target_pairs={{0,28},{4,0},{8,4},{12,8},{16,12},{20,16},{24,20},{28,24},{1,29},{... | collective-permute-start | bytes 442376 | tf_op jit(solution)/shard_map/ppermute | solution.py:318
  180.8 3.0 collective-permute-done.20.top.refs_5_
  186.9 2.4 collective-permute-start.23
  189.3 10.0 %forward_inner.5 = (f32[256,128]{1,0:T(8,128)}, f32[256,128]{1,0:T(8,128)}, f32[2,72,128]{2,1,0:T(8,128)}, f32[2,72,128]{2,1,0:T(8,128)}, f32[8,128]{1,0:T(8,128)}) custom-call(s32[768]{0:T(1024)} %reshape.19.refs_0_, f32[256,128]{1,0:T(8,128)} %get-tuple-element.173.first.refs_1_, f32[256,128]{1,0:T(8,128)} %get-tuple-element.174.refs_2_, ...), custom_call_target="tpu_custom_call" | custom-call | flops 33554432 | bytes 3670016 | tf_op jit(solution)/shard_map/forward_inner/pallas_call | solution.py:260
  200.1 11.3 %forward_outer.5 = (f32[256,128]{1,0:T(8,128)}, f32[256,128]{1,0:T(8,128)}, f32[4,72,128]{2,1,0:T(8,128)}, f32[4,72,128]{2,1,0:T(8,128)}, f32[8,128]{1,0:T(8,128)}) custom-call(s32[768]{0:T(1024)} %reshape.19.refs_0_, f32[256,128]{1,0:T(8,128)} %get-tuple-element.173.first.refs_1_, f32[256,128]{1,0:T(8,128)} %get-tuple-element.174.refs_2_, ...), custom_call_target="tpu_custom_call" | custom-call | flops 33554432 | bytes 3670016 | tf_op jit(solution)/shard_map/forward_outer/pallas_call | solution.py:260
  211.5 3.5 %collective-permute-start.25 = (f32[4,72,128]{2,1,0:T(8,128)}, f32[4,72,128]{2,1,0:T(8,128)S(1)}, u32[]{:S(2)}, u32[]{:S(2)}) collective-permute-start(f32[4,72,128]{2,1,0:T(8,128)} %get-tuple-element.192), channel_id=1, source_target_pairs={{0,28},{4,0},{8,4},{12,8},{16,12},{20,16},{24,20},{28,24},{1,29},{... | collective-permute-start | bytes 442376 | tf_op jit(solution)/shard_map/ppermute | solution.py:318
  215.0 4.5 %collective-permute-done.24.top.refs_5_ = f32[4,72,128]{2,1,0:T(8,128)S(1)} collective-permute-done((f32[4,72,128]{2,1,0:T(8,128)}, f32[4,72,128]{2,1,0:T(8,128)S(1)}, u32[]{:S(2)}, u32[]{:S(2)}) %collective-permute-start.24) | collective-permute-done | bytes 147488 | tf_op jit(solution)/shard_map/ppermute | solution.py:318
  222.5 2.6 collective-permute-start.27
  225.1 10.0 %forward_inner.6 = (f32[256,128]{1,0:T(8,128)}, f32[256,128]{1,0:T(8,128)}, f32[2,72,128]{2,1,0:T(8,128)}, f32[2,72,128]{2,1,0:T(8,128)}, f32[8,128]{1,0:T(8,128)}) custom-call(s32[768]{0:T(1024)} %reshape.19.refs_0_, f32[256,128]{1,0:T(8,128)} %get-tuple-element.187.first.refs_1_, f32[256,128]{1,0:T(8,128)} %get-tuple-element.188.refs_2_, ...), custom_call_target="tpu_custom_call" | custom-call | flops 33554432 | bytes 3670016 | tf_op jit(solution)/shard_map/forward_inner/pallas_call | solution.py:260
  236.0 11.4 %forward_outer.6 = (f32[256,128]{1,0:T(8,128)}, f32[256,128]{1,0:T(8,128)}, f32[4,72,128]{2,1,0:T(8,128)}, f32[4,72,128]{2,1,0:T(8,128)}, f32[8,128]{1,0:T(8,128)}) custom-call(s32[768]{0:T(1024)} %reshape.19.refs_0_, f32[256,128]{1,0:T(8,128)} %get-tuple-element.187.first.refs_1_, f32[256,128]{1,0:T(8,128)} %get-tuple-element.188.refs_2_, ...), custom_call_target="tpu_custom_call" | custom-call | flops 33554432 | bytes 3670016 | tf_op jit(solution)/shard_map/forward_outer/pallas_call | solution.py:260
  247.4 3.5 %collective-permute-start.29 = (f32[4,72,128]{2,1,0:T(8,128)}, f32[4,72,128]{2,1,0:T(8,128)S(1)}, u32[]{:S(2)}, u32[]{:S(2)}) collective-permute-start(f32[4,72,128]{2,1,0:T(8,128)} %get-tuple-element.206), channel_id=1, source_target_pairs={{0,28},{4,0},{8,4},{12,8},{16,12},{20,16},{24,20},{28,24},{1,29},{... | collective-permute-start | bytes 442376 | tf_op jit(solution)/shard_map/ppermute | solution.py:318
  254.9 1.9 columns.15
  257.6 2.1 collective-permute-start.31
  261.6 10.0 %forward_inner.7 = (f32[256,128]{1,0:T(8,128)}, f32[256,128]{1,0:T(8,128)}, f32[2,72,128]{2,1,0:T(8,128)}, f32[2,72,128]{2,1,0:T(8,128)}, f32[8,128]{1,0:T(8,128)}) custom-call(s32[768]{0:T(1024)} %reshape.19.refs_0_, f32[256,128]{1,0:T(8,128)} %get-tuple-element.201.first.refs_1_, f32[256,128]{1,0:T(8,128)} %get-tuple-element.202.refs_2_, ...), custom_call_target="tpu_custom_call" | custom-call | flops 33554432 | bytes 3670016 | tf_op jit(solution)/shard_map/forward_inner/pallas_call | solution.py:260
  272.3 11.3 %forward_outer.7 = (f32[256,128]{1,0:T(8,128)}, f32[256,128]{1,0:T(8,128)}, f32[4,72,128]{2,1,0:T(8,128)}, f32[4,72,128]{2,1,0:T(8,128)}, f32[8,128]{1,0:T(8,128)}) custom-call(s32[768]{0:T(1024)} %reshape.19.refs_0_, f32[256,128]{1,0:T(8,128)} %get-tuple-element.201.first.refs_1_, f32[256,128]{1,0:T(8,128)} %get-tuple-element.202.refs_2_, ...), custom_call_target="tpu_custom_call" | custom-call | flops 33554432 | bytes 3670016 | tf_op jit(solution)/shard_map/forward_outer/pallas_call | solution.py:260
  285.0 2.5 pad_maximum_fusion.1
  288.0 3.0 collective-permute-done.32
  291.1 2.5 fusion.9
  293.6 2.0 collective-permute-start.33
  297.2 2.5 fusion.10
  300.9 3.6 %collective-permute-done.35 = f32[4]{0:T(128)S(1)} collective-permute-done((f32[4]{0:T(128)S(1)}, f32[4]{0:T(128)S(1)}, u32[]{:S(2)}, u32[]{:S(2)}) %collective-permute-start.35) | collective-permute-done | bytes 48 | tf_op jit(solution)/shard_map/ppermute | solution.py:338
  304.4 4.5 %collective-permute-done.36 = f32[4]{0:T(128)S(1)} collective-permute-done((f32[4]{0:T(128)S(1)}, f32[4]{0:T(128)S(1)}, u32[]{:S(2)}, u32[]{:S(2)}) %collective-permute-start.36) | collective-permute-done | bytes 48 | tf_op jit(solution)/shard_map/ppermute | solution.py:338
  (162 shorter events, 46.1 us)
Async XLA Ops:
  2.6 7.7 %collective-permute-start = (f32[4,72,128]{2,1,0:T(8,128)}, f32[4,72,128]{2,1,0:T(8,128)S(1)}, u32[]{:S(2)}, u32[]{:S(2)}) collective-permute-start(f32[4,72,128]{2,1,0:T(8,128)} %get-tuple-element.119), channel_id=1, source_target_pairs={{0,4},{4,8},{8,12},{12,16},{16,20},{20,24},{24,28},{28,0},{1,5},{5... | collective-permute-start | bytes 442376 | tf_op jit(solution)/shard_map/ppermute | solution.py:318
  3.1 7.2 %collective-permute-start.1 = (f32[4,72,128]{2,1,0:T(8,128)}, f32[4,72,128]{2,1,0:T(8,128)S(1)}, u32[]{:S(2)}, u32[]{:S(2)}) collective-permute-start(f32[4,72,128]{2,1,0:T(8,128)} %get-tuple-element.120), channel_id=1, source_target_pairs={{0,28},{4,0},{8,4},{12,8},{16,12},{20,16},{24,20},{28,24},{1,29},{... | collective-permute-start | bytes 442376 | tf_op jit(solution)/shard_map/ppermute | solution.py:318
  12.8 14.6 %collective-permute-start.2 = (f32[400,128]{1,0:T(8,128)}, f32[400,128]{1,0:T(8,128)S(1)}, u32[]{:S(2)}, u32[]{:S(2)}) collective-permute-start(f32[400,128]{1,0:T(8,128)} %get-tuple-element.121), channel_id=1, source_target_pairs={{0,1},{1,2},{2,3},{3,0},{4,5},{5,6},{6,7},{7,4},{8,9},{9,10},{10,1... | collective-permute-start | bytes 614408 | tf_op jit(solution)/shard_map/ppermute | solution.py:318
  14.8 12.7 %collective-permute-start.3 = (f32[400,128]{1,0:T(8,128)}, f32[400,128]{1,0:T(8,128)S(1)}, u32[]{:S(2)}, u32[]{:S(2)}) collective-permute-start(f32[400,128]{1,0:T(8,128)} %get-tuple-element.122), channel_id=1, source_target_pairs={{0,3},{1,0},{2,1},{3,2},{4,7},{5,4},{6,5},{7,6},{8,11},{9,8},{10,9... | collective-permute-start | bytes 614408 | tf_op jit(solution)/shard_map/ppermute | solution.py:318
  40.0 7.5 %collective-permute-start.4 = (f32[4,72,128]{2,1,0:T(8,128)}, f32[4,72,128]{2,1,0:T(8,128)S(1)}, u32[]{:S(2)}, u32[]{:S(2)}) collective-permute-start(f32[4,72,128]{2,1,0:T(8,128)} %get-tuple-element.129), channel_id=1, source_target_pairs={{0,4},{4,8},{8,12},{12,16},{16,20},{20,24},{24,28},{28,0},{1,5},{5... | collective-permute-start | bytes 442376 | tf_op jit(solution)/shard_map/ppermute | solution.py:318
  41.0 6.5 %collective-permute-start.5 = (f32[4,72,128]{2,1,0:T(8,128)}, f32[4,72,128]{2,1,0:T(8,128)S(1)}, u32[]{:S(2)}, u32[]{:S(2)}) collective-permute-start(f32[4,72,128]{2,1,0:T(8,128)} %get-tuple-element.130), channel_id=1, source_target_pairs={{0,28},{4,0},{8,4},{12,8},{16,12},{20,16},{24,20},{28,24},{1,29},{... | collective-permute-start | bytes 442376 | tf_op jit(solution)/shard_map/ppermute | solution.py:318
  50.2 13.3 %collective-permute-start.6 = (f32[400,128]{1,0:T(8,128)}, f32[400,128]{1,0:T(8,128)S(1)}, u32[]{:S(2)}, u32[]{:S(2)}) collective-permute-start(f32[400,128]{1,0:T(8,128)} %get-tuple-element.131), channel_id=1, source_target_pairs={{0,1},{1,2},{2,3},{3,0},{4,5},{5,6},{6,7},{7,4},{8,9},{9,10},{10,1... | collective-permute-start | bytes 614408 | tf_op jit(solution)/shard_map/ppermute | solution.py:318
  51.7 11.8 %collective-permute-start.7 = (f32[400,128]{1,0:T(8,128)}, f32[400,128]{1,0:T(8,128)S(1)}, u32[]{:S(2)}, u32[]{:S(2)}) collective-permute-start(f32[400,128]{1,0:T(8,128)} %get-tuple-element.132), channel_id=1, source_target_pairs={{0,3},{1,0},{2,1},{3,2},{4,7},{5,4},{6,5},{7,6},{8,11},{9,8},{10,9... | collective-permute-start | bytes 614408 | tf_op jit(solution)/shard_map/ppermute | solution.py:318
  76.0 7.4 %collective-permute-start.8 = (f32[4,72,128]{2,1,0:T(8,128)}, f32[4,72,128]{2,1,0:T(8,128)S(1)}, u32[]{:S(2)}, u32[]{:S(2)}) collective-permute-start(f32[4,72,128]{2,1,0:T(8,128)} %get-tuple-element.139), channel_id=1, source_target_pairs={{0,4},{4,8},{8,12},{12,16},{16,20},{20,24},{24,28},{28,0},{1,5},{5... | collective-permute-start | bytes 442376 | tf_op jit(solution)/shard_map/ppermute | solution.py:318
  76.1 7.3 %collective-permute-start.9 = (f32[4,72,128]{2,1,0:T(8,128)}, f32[4,72,128]{2,1,0:T(8,128)S(1)}, u32[]{:S(2)}, u32[]{:S(2)}) collective-permute-start(f32[4,72,128]{2,1,0:T(8,128)} %get-tuple-element.140), channel_id=1, source_target_pairs={{0,28},{4,0},{8,4},{12,8},{16,12},{20,16},{24,20},{28,24},{1,29},{... | collective-permute-start | bytes 442376 | tf_op jit(solution)/shard_map/ppermute | solution.py:318
  86.0 13.4 %collective-permute-start.10 = (f32[400,128]{1,0:T(8,128)}, f32[400,128]{1,0:T(8,128)S(1)}, u32[]{:S(2)}, u32[]{:S(2)}) collective-permute-start(f32[400,128]{1,0:T(8,128)} %get-tuple-element.141), channel_id=1, source_target_pairs={{0,1},{1,2},{2,3},{3,0},{4,5},{5,6},{6,7},{7,4},{8,9},{9,10},{10,1... | collective-permute-start | bytes 614408 | tf_op jit(solution)/shard_map/ppermute | solution.py:318
  86.8 12.6 %collective-permute-start.11 = (f32[400,128]{1,0:T(8,128)}, f32[400,128]{1,0:T(8,128)S(1)}, u32[]{:S(2)}, u32[]{:S(2)}) collective-permute-start(f32[400,128]{1,0:T(8,128)} %get-tuple-element.142), channel_id=1, source_target_pairs={{0,3},{1,0},{2,1},{3,2},{4,7},{5,4},{6,5},{7,6},{8,11},{9,8},{10,9... | collective-permute-start | bytes 614408 | tf_op jit(solution)/shard_map/ppermute | solution.py:318
  111.9 9.1 %collective-permute-start.12 = (f32[4,72,128]{2,1,0:T(8,128)}, f32[4,72,128]{2,1,0:T(8,128)S(1)}, u32[]{:S(2)}, u32[]{:S(2)}) collective-permute-start(f32[4,72,128]{2,1,0:T(8,128)} %get-tuple-element.149), channel_id=1, source_target_pairs={{0,4},{4,8},{8,12},{12,16},{16,20},{20,24},{24,28},{28,0},{1,5},{5... | collective-permute-start | bytes 442376 | tf_op jit(solution)/shard_map/ppermute | solution.py:318
  112.0 9.1 %collective-permute-start.13 = (f32[4,72,128]{2,1,0:T(8,128)}, f32[4,72,128]{2,1,0:T(8,128)S(1)}, u32[]{:S(2)}, u32[]{:S(2)}) collective-permute-start(f32[4,72,128]{2,1,0:T(8,128)} %get-tuple-element.150), channel_id=1, source_target_pairs={{0,28},{4,0},{8,4},{12,8},{16,12},{20,16},{24,20},{28,24},{1,29},{... | collective-permute-start | bytes 442376 | tf_op jit(solution)/shard_map/ppermute | solution.py:318
  117.5 9.1 %collective-permute-start.16 = (f32[4,72,128]{2,1,0:T(8,128)}, f32[4,72,128]{2,1,0:T(8,128)S(1)}, u32[]{:S(2)}, u32[]{:S(2)}) collective-permute-start(f32[4,72,128]{2,1,0:T(8,128)} %get-tuple-element.163), channel_id=1, source_target_pairs={{0,4},{4,8},{8,12},{12,16},{16,20},{20,24},{24,28},{28,0},{1,5},{5... | collective-permute-start | bytes 442376 | tf_op jit(solution)/shard_map/ppermute | solution.py:318
  117.5 9.1 %collective-permute-start.17 = (f32[4,72,128]{2,1,0:T(8,128)}, f32[4,72,128]{2,1,0:T(8,128)S(1)}, u32[]{:S(2)}, u32[]{:S(2)}) collective-permute-start(f32[4,72,128]{2,1,0:T(8,128)} %get-tuple-element.164), channel_id=1, source_target_pairs={{0,28},{4,0},{8,4},{12,8},{16,12},{20,16},{24,20},{28,24},{1,29},{... | collective-permute-start | bytes 442376 | tf_op jit(solution)/shard_map/ppermute | solution.py:318
  123.6 29.0 %collective-permute-start.14 = (f32[400,128]{1,0:T(8,128)}, f32[400,128]{1,0:T(8,128)S(1)}, u32[]{:S(2)}, u32[]{:S(2)}) collective-permute-start(f32[400,128]{1,0:T(8,128)} %get-tuple-element.151), channel_id=1, source_target_pairs={{0,1},{1,2},{2,3},{3,0},{4,5},{5,6},{6,7},{7,4},{8,9},{9,10},{10,1... | collective-permute-start | bytes 614408 | tf_op jit(solution)/shard_map/ppermute | solution.py:318
  124.1 28.5 %collective-permute-start.15 = (f32[400,128]{1,0:T(8,128)}, f32[400,128]{1,0:T(8,128)S(1)}, u32[]{:S(2)}, u32[]{:S(2)}) collective-permute-start(f32[400,128]{1,0:T(8,128)} %get-tuple-element.152), channel_id=1, source_target_pairs={{0,3},{1,0},{2,1},{3,2},{4,7},{5,4},{6,5},{7,6},{8,11},{9,8},{10,9... | collective-permute-start | bytes 614408 | tf_op jit(solution)/shard_map/ppermute | solution.py:318
  129.1 36.0 %collective-permute-start.18 = (f32[400,128]{1,0:T(8,128)}, f32[400,128]{1,0:T(8,128)S(1)}, u32[]{:S(2)}, u32[]{:S(2)}) collective-permute-start(f32[400,128]{1,0:T(8,128)} %get-tuple-element.165), channel_id=1, source_target_pairs={{0,1},{1,2},{2,3},{3,0},{4,5},{5,6},{6,7},{7,4},{8,9},{9,10},{10,1... | collective-permute-start | bytes 614408 | tf_op jit(solution)/shard_map/ppermute | solution.py:318
  129.7 35.5 %collective-permute-start.19 = (f32[400,128]{1,0:T(8,128)}, f32[400,128]{1,0:T(8,128)S(1)}, u32[]{:S(2)}, u32[]{:S(2)}) collective-permute-start(f32[400,128]{1,0:T(8,128)} %get-tuple-element.166), channel_id=1, source_target_pairs={{0,3},{1,0},{2,1},{3,2},{4,7},{5,4},{6,5},{7,6},{8,11},{9,8},{10,9... | collective-permute-start | bytes 614408 | tf_op jit(solution)/shard_map/ppermute | solution.py:318
  177.2 6.6 %collective-permute-start.20 = (f32[4,72,128]{2,1,0:T(8,128)}, f32[4,72,128]{2,1,0:T(8,128)S(1)}, u32[]{:S(2)}, u32[]{:S(2)}) collective-permute-start(f32[4,72,128]{2,1,0:T(8,128)} %get-tuple-element.177), channel_id=1, source_target_pairs={{0,4},{4,8},{8,12},{12,16},{16,20},{20,24},{24,28},{28,0},{1,5},{5... | collective-permute-start | bytes 442376 | tf_op jit(solution)/shard_map/ppermute | solution.py:318
  177.2 6.6 %collective-permute-start.21 = (f32[4,72,128]{2,1,0:T(8,128)}, f32[4,72,128]{2,1,0:T(8,128)S(1)}, u32[]{:S(2)}, u32[]{:S(2)}) collective-permute-start(f32[4,72,128]{2,1,0:T(8,128)} %get-tuple-element.178), channel_id=1, source_target_pairs={{0,28},{4,0},{8,4},{12,8},{16,12},{20,16},{24,20},{28,24},{1,29},{... | collective-permute-start | bytes 442376 | tf_op jit(solution)/shard_map/ppermute | solution.py:318
  186.4 13.0 %collective-permute-start.22 = (f32[400,128]{1,0:T(8,128)}, f32[400,128]{1,0:T(8,128)S(1)}, u32[]{:S(2)}, u32[]{:S(2)}) collective-permute-start(f32[400,128]{1,0:T(8,128)} %get-tuple-element.179), channel_id=1, source_target_pairs={{0,1},{1,2},{2,3},{3,0},{4,5},{5,6},{6,7},{7,4},{8,9},{9,10},{10,1... | collective-permute-start | bytes 614408 | tf_op jit(solution)/shard_map/ppermute | solution.py:318
  186.9 12.5 %collective-permute-start.23 = (f32[400,128]{1,0:T(8,128)}, f32[400,128]{1,0:T(8,128)S(1)}, u32[]{:S(2)}, u32[]{:S(2)}) collective-permute-start(f32[400,128]{1,0:T(8,128)} %get-tuple-element.180), channel_id=1, source_target_pairs={{0,3},{1,0},{2,1},{3,2},{4,7},{5,4},{6,5},{7,6},{8,11},{9,8},{10,9... | collective-permute-start | bytes 614408 | tf_op jit(solution)/shard_map/ppermute | solution.py:318
  211.4 8.1 %collective-permute-start.24 = (f32[4,72,128]{2,1,0:T(8,128)}, f32[4,72,128]{2,1,0:T(8,128)S(1)}, u32[]{:S(2)}, u32[]{:S(2)}) collective-permute-start(f32[4,72,128]{2,1,0:T(8,128)} %get-tuple-element.191), channel_id=1, source_target_pairs={{0,4},{4,8},{8,12},{12,16},{16,20},{20,24},{24,28},{28,0},{1,5},{5... | collective-permute-start | bytes 442376 | tf_op jit(solution)/shard_map/ppermute | solution.py:318
  211.5 8.1 %collective-permute-start.25 = (f32[4,72,128]{2,1,0:T(8,128)}, f32[4,72,128]{2,1,0:T(8,128)S(1)}, u32[]{:S(2)}, u32[]{:S(2)}) collective-permute-start(f32[4,72,128]{2,1,0:T(8,128)} %get-tuple-element.192), channel_id=1, source_target_pairs={{0,28},{4,0},{8,4},{12,8},{16,12},{20,16},{24,20},{28,24},{1,29},{... | collective-permute-start | bytes 442376 | tf_op jit(solution)/shard_map/ppermute | solution.py:318
  222.2 13.0 %collective-permute-start.26 = (f32[400,128]{1,0:T(8,128)}, f32[400,128]{1,0:T(8,128)S(1)}, u32[]{:S(2)}, u32[]{:S(2)}) collective-permute-start(f32[400,128]{1,0:T(8,128)} %get-tuple-element.193), channel_id=1, source_target_pairs={{0,1},{1,2},{2,3},{3,0},{4,5},{5,6},{6,7},{7,4},{8,9},{9,10},{10,1... | collective-permute-start | bytes 614408 | tf_op jit(solution)/shard_map/ppermute | solution.py:318
  222.5 12.7 %collective-permute-start.27 = (f32[400,128]{1,0:T(8,128)}, f32[400,128]{1,0:T(8,128)S(1)}, u32[]{:S(2)}, u32[]{:S(2)}) collective-permute-start(f32[400,128]{1,0:T(8,128)} %get-tuple-element.194), channel_id=1, source_target_pairs={{0,3},{1,0},{2,1},{3,2},{4,7},{5,4},{6,5},{7,6},{8,11},{9,8},{10,9... | collective-permute-start | bytes 614408 | tf_op jit(solution)/shard_map/ppermute | solution.py:318
  235.9 15.1 %copy-start.38 = (f32[8,128]{1,0:T(8,128)S(1)}, f32[8,128]{1,0:T(8,128)}, u32[]{:S(2)}) copy-start(f32[8,128]{1,0:T(8,128)} %get-tuple-element.219) | copy-start | bytes 12292
  235.9 15.1 %copy-start.39 = (f32[8,128]{1,0:T(8,128)S(1)}, f32[8,128]{1,0:T(8,128)}, u32[]{:S(2)}) copy-start(f32[8,128]{1,0:T(8,128)} %get-tuple-element.220) | copy-start | bytes 12292
  235.9 15.7 %copy-start.32 = (f32[256,128]{1,0:T(8,128)S(1)}, f32[256,128]{1,0:T(8,128)}, u32[]{:S(2)}) copy-start(f32[256,128]{1,0:T(8,128)} %get-tuple-element.156) | copy-start | bytes 393220
  235.9 15.7 %copy-start.33 = (f32[256,128]{1,0:T(8,128)S(1)}, f32[256,128]{1,0:T(8,128)}, u32[]{:S(2)}) copy-start(f32[256,128]{1,0:T(8,128)} %get-tuple-element.157) | copy-start | bytes 393220
  235.9 15.7 %copy-start.34 = (f32[256,128]{1,0:T(8,128)S(1)}, f32[256,128]{1,0:T(8,128)}, u32[]{:S(2)}) copy-start(f32[256,128]{1,0:T(8,128)} %get-tuple-element.155) | copy-start | bytes 393220
  235.9 15.7 %copy-start.35 = (f32[256,128]{1,0:T(8,128)S(1)}, f32[256,128]{1,0:T(8,128)}, u32[]{:S(2)}) copy-start(f32[256,128]{1,0:T(8,128)} %get-tuple-element.158) | copy-start | bytes 393220
  235.9 23.8 %copy-start.40 = (f32[8,128]{1,0:T(8,128)S(1)}, f32[8,128]{1,0:T(8,128)}, u32[]{:S(2)}) copy-start(f32[8,128]{1,0:T(8,128)} %get-tuple-element.221) | copy-start | bytes 12292
  235.9 23.7 %copy-start.41 = (f32[8,128]{1,0:T(8,128)S(1)}, f32[8,128]{1,0:T(8,128)}, u32[]{:S(2)}) copy-start(f32[8,128]{1,0:T(8,128)} %get-tuple-element.222) | copy-start | bytes 12292
  235.9 24.4 %copy-start.42 = (f32[8,128]{1,0:T(8,128)S(1)}, f32[8,128]{1,0:T(8,128)}, u32[]{:S(2)}) copy-start(f32[8,128]{1,0:T(8,128)} %get-tuple-element.223) | copy-start | bytes 12292
  247.4 6.8 %collective-permute-start.28 = (f32[4,72,128]{2,1,0:T(8,128)}, f32[4,72,128]{2,1,0:T(8,128)S(1)}, u32[]{:S(2)}, u32[]{:S(2)}) collective-permute-start(f32[4,72,128]{2,1,0:T(8,128)} %get-tuple-element.205), channel_id=1, source_target_pairs={{0,4},{4,8},{8,12},{12,16},{16,20},{20,24},{24,28},{28,0},{1,5},{5... | collective-permute-start | bytes 442376 | tf_op jit(solution)/shard_map/ppermute | solution.py:318
  247.4 6.7 %collective-permute-start.29 = (f32[4,72,128]{2,1,0:T(8,128)}, f32[4,72,128]{2,1,0:T(8,128)S(1)}, u32[]{:S(2)}, u32[]{:S(2)}) collective-permute-start(f32[4,72,128]{2,1,0:T(8,128)} %get-tuple-element.206), channel_id=1, source_target_pairs={{0,28},{4,0},{8,4},{12,8},{16,12},{20,16},{24,20},{28,24},{1,29},{... | collective-permute-start | bytes 442376 | tf_op jit(solution)/shard_map/ppermute | solution.py:318
  256.7 14.8 %collective-permute-start.30 = (f32[400,128]{1,0:T(8,128)}, f32[400,128]{1,0:T(8,128)S(1)}, u32[]{:S(2)}, u32[]{:S(2)}) collective-permute-start(f32[400,128]{1,0:T(8,128)} %get-tuple-element.207), channel_id=1, source_target_pairs={{0,1},{1,2},{2,3},{3,0},{4,5},{5,6},{6,7},{7,4},{8,9},{9,10},{10,1... | collective-permute-start | bytes 614408 | tf_op jit(solution)/shard_map/ppermute | solution.py:318
  257.6 14.0 %collective-permute-start.31 = (f32[400,128]{1,0:T(8,128)}, f32[400,128]{1,0:T(8,128)S(1)}, u32[]{:S(2)}, u32[]{:S(2)}) collective-permute-start(f32[400,128]{1,0:T(8,128)} %get-tuple-element.208), channel_id=1, source_target_pairs={{0,3},{1,0},{2,1},{3,2},{4,7},{5,4},{6,5},{7,6},{8,11},{9,8},{10,9... | collective-permute-start | bytes 614408 | tf_op jit(solution)/shard_map/ppermute | solution.py:318
  272.3 42.9 %copy-start.36 = (f32[256,128]{1,0:T(8,128)S(1)}, f32[256,128]{1,0:T(8,128)}, u32[]{:S(2)}) copy-start(f32[256,128]{1,0:T(8,128)} %get-tuple-element.216) | copy-start | bytes 393220
  272.3 42.9 %copy-start.37 = (f32[256,128]{1,0:T(8,128)S(1)}, f32[256,128]{1,0:T(8,128)}, u32[]{:S(2)}) copy-start(f32[256,128]{1,0:T(8,128)} %get-tuple-element.217) | copy-start | bytes 393220
  287.5 3.6 %collective-permute-start.32 = (f32[4]{0:T(128)S(1)}, f32[4]{0:T(128)S(1)}, u32[]{:S(2)}, u32[]{:S(2)}) collective-permute-start(f32[4]{0:T(128)S(1)} %pad_maximum_fusion.1), channel_id=1, source_target_pairs={{0,1},{1,0},{2,3},{3,2},{4,5},{5,4},{6,7},{7,6},{8,9},{9,8},{10,11... | collective-permute-start | bytes 56 | tf_op jit(solution)/shard_map/ppermute | solution.py:338
  293.6 3.6 %collective-permute-start.33 = (f32[4]{0:T(128)S(1)}, f32[4]{0:T(128)S(1)}, u32[]{:S(2)}, u32[]{:S(2)}) collective-permute-start(f32[4]{0:T(128)S(1)} %fusion.9), channel_id=1, source_target_pairs={{0,2},{1,3},{2,0},{3,1},{4,6},{5,7},{6,4},{7,5},{8,10},{9,11},{10,... | collective-permute-start | bytes 56 | tf_op jit(solution)/shard_map/ppermute | solution.py:338
  299.7 1.2 collective-permute-start.34
  300.9 3.6 %collective-permute-start.35 = (f32[4]{0:T(128)S(1)}, f32[4]{0:T(128)S(1)}, u32[]{:S(2)}, u32[]{:S(2)}) collective-permute-start(f32[4]{0:T(128)S(1)} %add.144), channel_id=1, source_target_pairs={{0,8},{4,12},{8,0},{12,4},{16,24},{20,28},{24,16},{28,20},{1,9},{5... | collective-permute-start | bytes 56 | tf_op jit(solution)/shard_map/ppermute | solution.py:338
  304.4 4.5 %collective-permute-start.36 = (f32[4]{0:T(128)S(1)}, f32[4]{0:T(128)S(1)}, u32[]{:S(2)}, u32[]{:S(2)}) collective-permute-start(f32[4]{0:T(128)S(1)} %add.145), channel_id=1, source_target_pairs={{0,16},{4,20},{8,24},{12,28},{16,0},{20,4},{24,8},{28,12},{1,17},{... | collective-permute-start | bytes 56 | tf_op jit(solution)/shard_map/ppermute | solution.py:338
  (33 other events, 33.7 us)

commit v2 on v1

--- a/solution.py
+++ b/solution.py
@@ -139,7 +139,7 @@
         bottom[tile] = inner_bottom[tile - 1]
 
 
-def step_kernel(wanted, count, moment_entry, cost_entry, rows, is_backward, is_outer, *refs):
+def step_kernel(wanted, count, moment_entry, cost_entry, moment, rows, is_backward, is_outer, *refs):
     refs = list(refs)
     take = lambda n: [refs.pop(0) for _ in range(n)]
     (table,) = take(1)
@@ -152,6 +152,7 @@
         crowding = take(len(wanted))
     else:
         ramps, inverse = take(2)
+        earlier, inner_mass = take(2) if is_outer else (None, None)
     values = take(len(wanted))
     edge_top, edge_bottom = take(2)
     if is_backward:
@@ -201,6 +202,10 @@
     @pl.when(pl.program_id(0) == pl.num_programs(0) - 1)
     def _():
         edges_out(values, inner_top, inner_bottom, edge_top, edge_bottom)
+        if is_outer and not is_backward:
+            place = lax.broadcasted_iota(jnp.int32, (SUBLANES, LANES), 0) * LANES
+            place += lax.broadcasted_iota(jnp.int32, (SUBLANES, LANES), 1)
+            mass[...] = jnp.where(place == moment, jnp.sum(mass[...] + inner_mass[...]), earlier[...])
 
 
 def padded_rows(height):
@@ -214,7 +219,7 @@
     return height
 
 
-def step(wanted, entry, cost_entry, controls, moment, table, tiles, halo, sides, inner, fractions, backward, forward):
+def step(wanted, entry, cost_entry, controls, moment, table, tiles, halo, sides, inner, fractions, backward, forward, which, sums):
     is_backward, is_outer = backward is not None, sides is not None
     height = tiles[0].shape[0]
     count = len(tiles)
@@ -222,7 +227,7 @@
     rows = row_chunk(height)
     whole = lambda *shape: pl.BlockSpec(shape, lambda c: (0,) * len(shape))
     smem = pl.BlockSpec(memory_space=pltpu.SMEM)
-    edge = whole(count, ROW_HALO, LANES)
+    edge = pl.BlockSpec((count, ROW_HALO, LANES), lambda c: (which, 0, 0))
     inner_edge = whole(count - 2, ROW_HALO, LANES)
     fraction = [
         pl.BlockSpec((1, 2, rows, LANES), functools.partial(lambda t, c: (moment, 0, c, t), tile)) for tile in wanted
@@ -247,6 +252,9 @@
     else:
         args += [*forward]
         specs += [ramp, inverse]
+        if is_outer:
+            args += [*sums]
+            specs += [whole(SUBLANES, LANES)] * 2
 
     edge_count = count if is_outer else group
     outs = [f32(height, LANES)] * group + [f32(edge_count, ROW_HALO, LANES)] * 2
@@ -258,7 +266,7 @@
         outs += [f32(SUBLANES, LANES)]
         out_specs += [whole(SUBLANES, LANES)]
     results = pl.pallas_call(
-        functools.partial(step_kernel, wanted, count, entry, cost_entry, rows, is_backward, is_outer),
+        functools.partial(step_kernel, wanted, count, entry, cost_entry, moment, rows, is_backward, is_outer),
         grid=(height // rows,),
         in_specs=specs,
         out_specs=out_specs,
@@ -278,39 +286,52 @@
     return results[:group], results[group : group + 2], results[group + 2 :]
 
 
-def split_kernel(cells, *outs):
-    *tiles, top, bottom = outs
-    height = cells.shape[0]
+def split_kernel(fields, *refs):
+    cells, tiles, (top, bottom) = refs[:fields], refs[fields:-2], refs[-2:]
+    height = cells[0].shape[0]
     for n, tile in enumerate(tiles):
-        piece = cells[:, n * LANES : (n + 1) * LANES]
+        field, column = divmod(n, len(tiles) // fields)
+        piece = cells[field][:, column * LANES : (column + 1) * LANES]
         tile[...] = piece
         top[n] = piece[0:ROW_HALO, :]
         bottom[n] = piece[height - ROW_HALO : height, :]
 
 
-def split(cells):
-    height, breadth = cells.shape
+def split(*fields):
+    height, breadth = fields[0].shape
     count = breadth // LANES
     f32 = lambda *shape: jax.ShapeDtypeStruct(shape, jnp.float32)
     results = pl.pallas_call(
-        split_kernel,
-        out_shape=[f32(height, LANES)] * count + [f32(count, ROW_HALO, LANES)] * 2,
+        functools.partial(split_kernel, len(fields)),
+        out_shape=[f32(height, LANES)] * (count * len(fields)) + [f32(count * len(fields), ROW_HALO, LANES)] * 2,
         name="split",
-    )(cells)
-    return results[:count], results[count:]
-
-
-def columns_kernel(top, bottom, first, last, first_out, last_out):
+    )(*fields)
+    return [results[n * count : (n + 1) * count] for n in range(len(fields))], results[-2:]
+
+
+def columns_kernel(places, top, bottom, first, last, first_out, last_out, ready):
     height = first.shape[0]
-    for tile, cells, out in ((0, first, first_out), (top.shape[0] - 1, last, last_out)):
-        out[0:ROW_HALO, :] = top[tile]
-        out[ROW_HALO : ROW_HALO + height, :] = cells[...]
-        out[ROW_HALO + height : 2 * ROW_HALO + height, :] = bottom[tile]
-
-
-def columns(halo, first, last):
-    out = jax.ShapeDtypeStruct((first.shape[0] + 2 * ROW_HALO, LANES), jnp.float32)
-    return pl.pallas_call(columns_kernel, out_shape=[out, out], name="columns")(*halo, first, last)
+    copies = []
+    for place, tile, out in zip(places, (first, last), (first_out, last_out)):
+        parts = ((top.at[place], 0, ROW_HALO), (tile, ROW_HALO, height), (bottom.at[place], ROW_HALO + height, ROW_HALO))
+        for source, start, rows in parts:
+            copies.append(pltpu.make_async_copy(source, out.at[pl.ds(start, rows), :], ready.at[len(copies)]))
+    for copy in copies:
+        copy.start()
+    for copy in copies:
+        copy.wait()
+
+
+def columns(halo, tiles, which):
+    places = (which * len(tiles), which * len(tiles) + len(tiles) - 1)
+    out = jax.ShapeDtypeStruct((tiles[0].shape[0] + 2 * ROW_HALO, LANES), jnp.float32)
+    return pl.pallas_call(
+        functools.partial(columns_kernel, places),
+        in_specs=[pl.BlockSpec(memory_space=pl.ANY)] * 4,
+        out_shape=[out, out],
+        scratch_shapes=[pltpu.SemaphoreType.DMA((6,))],
+        name="columns",
+    )(*halo, tiles[0], tiles[-1])
 
 
 def passed(cells, axis, distance):
@@ -322,8 +343,8 @@
     return passed(edges[1], "gx", 1), passed(edges[0], "gx", -1)
 
 
-def column_halo(halo, tiles):
-    first, last = columns(halo, tiles[0], tiles[-1])
+def column_halo(halo, tiles, which=0):
+    first, last = columns(halo, tiles, which)
     return passed(last, "gy", 1), passed(first, "gy", -1)
 
 
@@ -335,8 +356,15 @@
             continue
         distance = 1
         while distance < count:
-            sums = sums + lax.ppermute(sums, axis, [(i, i ^ distance) for i in range(count)])
-            distance *= 2
+            left_over = count // distance
+            radix = 2 if left_over.bit_length() % 2 == 0 else 4
+            there = [
+                lax.ppermute(sums, axis, [(i, i ^ (j * distance)) for i in range(count)]) for j in range(1, radix)
+            ]
+            sums = sums + there[0]
+            if radix == 4:
+                sums = sums + (there[1] + there[2])
+            distance *= radix
     return sums
 
 
@@ -349,35 +377,48 @@
     costs = time_step * control_cost.reshape(-1)
     inside, outside = tuple(range(1, count - 1)), (0, count - 1)
 
-    def both_groups(tiles, halo, entry, moment, backward, policy):
-        sides = column_halo(halo, tiles)
+    def both_groups(tiles, halo, sides, entry, moment, backward, policy, which=0, sums=None):
         common = (entry, moment * controls, controls, moment, table, tiles, halo)
         inner, inner_edges, inner_rest = step(
-            inside, *common, None, None, fractions, backward, None if policy is None else policy[0]
+            inside, *common, None, None, fractions, backward, None if policy is None else policy[0], which, None
         )
         outer, edges, outer_rest = step(
-            outside, *common, sides, inner_edges, fractions, backward, None if policy is None else policy[1]
+            outside,
+            *common,
+            sides,
+            inner_edges,
+            fractions,
+            backward,
+            None if policy is None else policy[1],
+            which,
+            None if policy is None else (sums, *inner_rest),
         )
         return [outer[0], *inner, outer[1]], edges, (inner_rest, outer_rest)
 
-    tiles, edges = split(terminal)
+    (tiles, dense), edges = split(terminal, density)
+    first_halo = row_halo(edges)
+    halo = first_halo
     policies = [None] * steps_count
     for moment in reversed(range(steps_count)):
+        if moment < steps_count - 1:
+            halo = row_halo(edges)
+        sides = column_halo(halo, tiles)
         entry = moment * controls * FIELDS
-        tiles, edges, policies[moment] = both_groups(
-            tiles, row_halo(edges), entry, moment, (costs, crowding), None
+        tiles, edges, policies[moment] = both_groups(tiles, halo, sides, entry, moment, (costs, crowding), None)
+    value = jnp.concatenate(tiles, axis=1)
+
+    tiles, halo = dense, first_halo
+    sums = jnp.zeros((SUBLANES, LANES), jnp.float32)
+    for moment in range(steps_count):
+        if moment > 0:
+            halo = row_halo(edges)
+        which = 0 if moment else 1
+        sides = column_halo(halo, tiles, which)
+        entry = (steps_count + moment) * controls * FIELDS
+        tiles, edges, (_, (sums,)) = both_groups(
+            tiles, halo, sides, entry, moment, None, policies[moment], which, sums
         )
-    value = jnp.concatenate(tiles, axis=1)
-
-    tiles, edges = split(density)
-    local_sums = []
-    for moment in range(steps_count):
-        entry = (steps_count + moment) * controls * FIELDS
-        tiles, edges, ((inner_mass,), (outer_mass,)) = both_groups(
-            tiles, row_halo(edges), entry, moment, None, policies[moment]
-        )
-        local_sums.append(jnp.sum(inner_mass + outer_mass))
-    totals = everywhere(jnp.stack(local_sums)) / cells
+    totals = everywhere(sums)[0, :steps_count] / cells
     masses = []
     scale = jnp.float32(1.0)
     for moment in range(steps_count):

time: 320 us -> 309 us (0.966)
  other arithmetic: 16.9 us -> 5.52 us
    ppermute x32 -> x30, waiting for transfers between devices: 18.5 us -> 26.2 us  [passed(): lax.ppermute(cells, axis, [(i, (i + distance) % count) for i in range(cou...]
    ppermute x5 -> x7, waiting for transfers between devices: 13.8 us -> 6.24 us  [everywhere(): lax.ppermute(sums, axis, [(i, i ^ j * distance) for i in range(count)])]
    ppermute x5 -> x7, starting transfers between devices: 2.56 us -> 7.95 us  [everywhere(): lax.ppermute(sums, axis, [(i, i ^ j * distance) for i in range(count)])]
    add x4 -> x3, other arithmetic: 5.07 us -> 0.69 us  [the longest x2 0.69 us: everywhere(): sums = sums + (there[1] + there[2])]
    reduce_sum x4 -> x0, other arithmetic: 3.76 us -> none  [shards(): local_sums.append(jnp.sum(inner_mass + outer_mass))]
    ppermute x32 -> x30, starting transfers between devices: 53 us -> 50 us  [passed(): lax.ppermute(cells, axis, [(i, (i + distance) % count) for i in range(cou...]
    pallas_call x10 -> x9, Pallas kernels: 19 us -> 17.1 us  [the longest x8 14.7 us: columns(): pl.pallas_call(functools.partial(columns_kernel, places), in_specs=[pl.Bl...]
    unnamed x88 -> x74, local copies, waits for them, and re-layouts: 11.6 us -> 10.2 us
  transfers between devices with their start and end apart: 37 -> 37, of which waited for: 11 -> 14; matrix products, arithmetic and copies ran while one was open for 2% -> 1% of each run, Pallas kernels for 31% -> 31%
where the time goes in v2:
time: 309 us; the launch traced here: 306 us
  Pallas kernels  192 us (62%)
  starting transfers between devices  58 us (19%)
  waiting for transfers between devices  32.4 us (10%)
  local copies, waits for them, and re-layouts  12.8 us (4%)
  between operations  5.63 us (2%)
  other arithmetic  5.52 us (2%)
    pallas_call x16, Pallas kernels, step(): pl.pallas_call(functools.partial(step_kernel, wanted, count, entry, cost_...  175 us
    ppermute x30, starting transfers between devices, passed(): lax.ppermute(cells, axis, [(i, (i + distance) % count) for i in range(cou...  50 us
    ppermute x30, waiting for transfers between devices, passed(): lax.ppermute(cells, axis, [(i, (i + distance) % count) for i in range(cou...  26.2 us
    pallas_call x8, Pallas kernels, columns(): pl.pallas_call(functools.partial(columns_kernel, places), in_specs=[pl.Bl...  14.7 us
    unnamed x74, local copies, waits for them, and re-layouts  10.2 us
    ppermute x7, starting transfers between devices, everywhere(): lax.ppermute(sums, axis, [(i, i ^ j * distance) for i in range(count)])  7.95 us
    ppermute x7, waiting for transfers between devices, everywhere(): lax.ppermute(sums, axis, [(i, i ^ j * distance) for i in range(count)])  6.24 us
  transfers between devices with their start and end apart: 37, of which 14 were waited for; matrix products, arithmetic and copies ran while one was open for 1% of the time, Pallas kernels for 31%

profile of v2, /device:TPU:0, one launch (start us, length us, event | category | flops | bytes accessed | tf_op | source)
XLA Modules:
  0.0 306.5 jit_solution(10913688217345920757)
XLA Ops:
  0.6 2.4 split.1
  3.5 4.0 %collective-permute-start.1 = (f32[8,72,128]{2,1,0:T(8,128)}, f32[8,72,128]{2,1,0:T(8,128)S(1)}, u32[]{:S(2)}, u32[]{:S(2)}) collective-permute-start(f32[8,72,128]{2,1,0:T(8,128)} %get-tuple-element.118), channel_id=1, source_target_pairs={{0,28},{4,0},{8,4},{12,8},{16,12},{20,16},{24,20},{28,24},{1,29},{... | collective-permute-start | bytes 884744 | tf_op jit(solution)/shard_map/ppermute | solution.py:339
  9.2 3.5 %collective-permute-done.top.refs_6_.refs_5_ = f32[8,72,128]{2,1,0:T(8,128)S(1)} collective-permute-done((f32[8,72,128]{2,1,0:T(8,128)}, f32[8,72,128]{2,1,0:T(8,128)S(1)}, u32[]{:S(2)}, u32[]{:S(2)}) %collective-permute-start) | collective-permute-done | bytes 294944 | tf_op jit(solution)/shard_map/ppermute | solution.py:339
  14.0 1.9 columns.8
  15.8 2.1 collective-permute-start.2
  19.6 10.4 %backward_inner.4 = (f32[256,128]{1,0:T(8,128)}, f32[256,128]{1,0:T(8,128)}, f32[2,72,128]{2,1,0:T(8,128)}, f32[2,72,128]{2,1,0:T(8,128)}, f32[2,8,256,128]{3,2,1,0:T(8,128)}, /*index=5*/f32[2,256,128]{2,1,0:T(8,128)}) custom-call(s32[768]{0:T(1024)} %reshape.28.refs_0_, f32[32]{0:T(128)} %mul.27.refs_1_, f32[256,128]{1,0:T(8,128)} %get-tuple-element.113.first.refs_2_, ...), custom_call_target="tpu_custom_call" | custom-call | flops 33554432 | bytes 3670016 | tf_op jit(solution)/shard_map/backward_inner/pallas_call | solution.py:268
  30.8 11.8 %backward_outer.4 = (f32[256,128]{1,0:T(8,128)}, f32[256,128]{1,0:T(8,128)}, f32[4,72,128]{2,1,0:T(8,128)}, f32[4,72,128]{2,1,0:T(8,128)}, f32[2,8,256,128]{3,2,1,0:T(8,128)}, /*index=5*/f32[2,256,128]{2,1,0:T(8,128)}) custom-call(s32[768]{0:T(1024)} %reshape.28.refs_0_, f32[32]{0:T(128)} %mul.27.refs_1_, f32[256,128]{1,0:T(8,128)} %get-tuple-element.113.first.refs_2_, ...), custom_call_target="tpu_custom_call" | custom-call | flops 33554432 | bytes 3670016 | tf_op jit(solution)/shard_map/backward_outer/pallas_call | solution.py:268
  44.2 2.0 collective-permute-start.5
  46.2 3.1 %collective-permute-done.4.top.refs_6_ = f32[4,72,128]{2,1,0:T(8,128)S(1)} collective-permute-done((f32[4,72,128]{2,1,0:T(8,128)}, f32[4,72,128]{2,1,0:T(8,128)S(1)}, u32[]{:S(2)}, u32[]{:S(2)}) %collective-permute-start.4) | collective-permute-done | bytes 147488 | tf_op jit(solution)/shard_map/ppermute | solution.py:339
  50.0 1.9 columns.9
  52.9 1.9 collective-permute-start.7
  54.9 10.5 %backward_inner.5 = (f32[256,128]{1,0:T(8,128)}, f32[256,128]{1,0:T(8,128)}, f32[2,72,128]{2,1,0:T(8,128)}, f32[2,72,128]{2,1,0:T(8,128)}, f32[2,8,256,128]{3,2,1,0:T(8,128)}, /*index=5*/f32[2,256,128]{2,1,0:T(8,128)}) custom-call(s32[768]{0:T(1024)} %reshape.28.refs_0_, f32[32]{0:T(128)} %mul.27.refs_1_, f32[256,128]{1,0:T(8,128)} %get-tuple-element.123.first.refs_2_, ...), custom_call_target="tpu_custom_call" | custom-call | flops 33554432 | bytes 3670016 | tf_op jit(solution)/shard_map/backward_inner/pallas_call | solution.py:268
  66.3 11.8 %backward_outer.5 = (f32[256,128]{1,0:T(8,128)}, f32[256,128]{1,0:T(8,128)}, f32[4,72,128]{2,1,0:T(8,128)}, f32[4,72,128]{2,1,0:T(8,128)}, f32[2,8,256,128]{3,2,1,0:T(8,128)}, /*index=5*/f32[2,256,128]{2,1,0:T(8,128)}) custom-call(s32[768]{0:T(1024)} %reshape.28.refs_0_, f32[32]{0:T(128)} %mul.27.refs_1_, f32[256,128]{1,0:T(8,128)} %get-tuple-element.123.first.refs_2_, ...), custom_call_target="tpu_custom_call" | custom-call | flops 33554432 | bytes 3670016 | tf_op jit(solution)/shard_map/backward_outer/pallas_call | solution.py:268
  78.6 3.0 collective-permute-start.9
  81.7 3.9 %collective-permute-done.8.top.refs_6_ = f32[4,72,128]{2,1,0:T(8,128)S(1)} collective-permute-done((f32[4,72,128]{2,1,0:T(8,128)}, f32[4,72,128]{2,1,0:T(8,128)S(1)}, u32[]{:S(2)}, u32[]{:S(2)}) %collective-permute-start.8) | collective-permute-done | bytes 147488 | tf_op jit(solution)/shard_map/ppermute | solution.py:339
  86.3 1.8 columns.10
  91.1 10.5 %backward_inner.6 = (f32[256,128]{1,0:T(8,128)}, f32[256,128]{1,0:T(8,128)}, f32[2,72,128]{2,1,0:T(8,128)}, f32[2,72,128]{2,1,0:T(8,128)}, f32[2,8,256,128]{3,2,1,0:T(8,128)}, /*index=5*/f32[2,256,128]{2,1,0:T(8,128)}) custom-call(s32[768]{0:T(1024)} %reshape.28.refs_0_, f32[32]{0:T(128)} %mul.27.refs_1_, f32[256,128]{1,0:T(8,128)} %get-tuple-element.133.first.refs_2_, ...), custom_call_target="tpu_custom_call" | custom-call | flops 33554432 | bytes 3670016 | tf_op jit(solution)/shard_map/backward_inner/pallas_call | solution.py:268
  102.3 11.8 %backward_outer.6 = (f32[256,128]{1,0:T(8,128)}, f32[256,128]{1,0:T(8,128)}, f32[4,72,128]{2,1,0:T(8,128)}, f32[4,72,128]{2,1,0:T(8,128)}, f32[2,8,256,128]{3,2,1,0:T(8,128)}, /*index=5*/f32[2,256,128]{2,1,0:T(8,128)}) custom-call(s32[768]{0:T(1024)} %reshape.28.refs_0_, f32[32]{0:T(128)} %mul.27.refs_1_, f32[256,128]{1,0:T(8,128)} %get-tuple-element.133.first.refs_2_, ...), custom_call_target="tpu_custom_call" | custom-call | flops 33554432 | bytes 3670016 | tf_op jit(solution)/shard_map/backward_outer/pallas_call | solution.py:268
  114.2 3.5 %collective-permute-start.13 = (f32[4,72,128]{2,1,0:T(8,128)}, f32[4,72,128]{2,1,0:T(8,128)S(1)}, u32[]{:S(2)}, u32[]{:S(2)}) collective-permute-start(f32[4,72,128]{2,1,0:T(8,128)} %get-tuple-element.148), channel_id=1, source_target_pairs={{0,28},{4,0},{8,4},{12,8},{16,12},{20,16},{24,20},{28,24},{1,29},{... | collective-permute-start | bytes 442376 | tf_op jit(solution)/shard_map/ppermute | solution.py:339
  117.7 3.8 %collective-permute-done.12.top.refs_6_ = f32[4,72,128]{2,1,0:T(8,128)S(1)} collective-permute-done((f32[4,72,128]{2,1,0:T(8,128)}, f32[4,72,128]{2,1,0:T(8,128)S(1)}, u32[]{:S(2)}, u32[]{:S(2)}) %collective-permute-start.12) | collective-permute-done | bytes 147488 | tf_op jit(solution)/shard_map/ppermute | solution.py:339
  122.3 1.8 columns.11
  124.8 2.3 collective-permute-start.15
  127.1 1.9 columns.12
  129.3 2.6 collective-permute-start.17
  132.0 10.5 %backward_inner.7 = (f32[256,128]{1,0:T(8,128)}, f32[256,128]{1,0:T(8,128)}, f32[2,72,128]{2,1,0:T(8,128)}, f32[2,72,128]{2,1,0:T(8,128)}, f32[2,8,256,128]{3,2,1,0:T(8,128)}, /*index=5*/f32[2,256,128]{2,1,0:T(8,128)}) custom-call(s32[768]{0:T(1024)} %reshape.28.refs_0_, f32[32]{0:T(128)} %mul.27.refs_1_, f32[256,128]{1,0:T(8,128)} %get-tuple-element.143.first.refs_2_, ...), custom_call_target="tpu_custom_call" | custom-call | flops 33554432 | bytes 3670016 | tf_op jit(solution)/shard_map/backward_inner/pallas_call | solution.py:268
  142.5 10.1 %forward_inner.4 = (f32[256,128]{1,0:T(8,128)}, f32[256,128]{1,0:T(8,128)}, f32[2,72,128]{2,1,0:T(8,128)}, f32[2,72,128]{2,1,0:T(8,128)}, f32[8,128]{1,0:T(8,128)}) custom-call(s32[768]{0:T(1024)} %reshape.28.refs_0_, f32[256,128]{1,0:T(8,128)} %get-tuple-element.157.first.refs_1_, f32[256,128]{1,0:T(8,128)} %get-tuple-element.158.refs_2_, ...), custom_call_target="tpu_custom_call" | custom-call | flops 33554432 | bytes 3670016 | tf_op jit(solution)/shard_map/forward_inner/pallas_call | solution.py:268
  153.4 11.8 %backward_outer.7 = (f32[256,128]{1,0:T(8,128)}, f32[256,128]{1,0:T(8,128)}, f32[4,72,128]{2,1,0:T(8,128)}, f32[4,72,128]{2,1,0:T(8,128)}, f32[2,8,256,128]{3,2,1,0:T(8,128)}, /*index=5*/f32[2,256,128]{2,1,0:T(8,128)}) custom-call(s32[768]{0:T(1024)} %reshape.28.refs_0_, f32[32]{0:T(128)} %mul.27.refs_1_, f32[256,128]{1,0:T(8,128)} %get-tuple-element.143.first.refs_2_, ...), custom_call_target="tpu_custom_call" | custom-call | flops 33554432 | bytes 3670016 | tf_op jit(solution)/shard_map/backward_outer/pallas_call | solution.py:268
  166.0 11.4 %forward_outer.4 = (f32[256,128]{1,0:T(8,128)}, f32[256,128]{1,0:T(8,128)}, f32[4,72,128]{2,1,0:T(8,128)}, f32[4,72,128]{2,1,0:T(8,128)}, f32[8,128]{1,0:T(8,128)}) custom-call(s32[768]{0:T(1024)} %reshape.28.refs_0_, f32[256,128]{1,0:T(8,128)} %get-tuple-element.157.first.refs_1_, f32[256,128]{1,0:T(8,128)} %get-tuple-element.158.refs_2_, ...), custom_call_target="tpu_custom_call" | custom-call | flops 33554432 | bytes 3670016 | tf_op jit(solution)/shard_map/forward_outer/pallas_call | solution.py:268
  177.4 3.5 %collective-permute-start.19 = (f32[4,72,128]{2,1,0:T(8,128)}, f32[4,72,128]{2,1,0:T(8,128)S(1)}, u32[]{:S(2)}, u32[]{:S(2)}) collective-permute-start(f32[4,72,128]{2,1,0:T(8,128)} %get-tuple-element.175), channel_id=1, source_target_pairs={{0,28},{4,0},{8,4},{12,8},{16,12},{20,16},{24,20},{28,24},{1,29},{... | collective-permute-start | bytes 442376 | tf_op jit(solution)/shard_map/ppermute | solution.py:339
  180.9 3.3 %collective-permute-done.18.top.refs_5_ = f32[4,72,128]{2,1,0:T(8,128)S(1)} collective-permute-done((f32[4,72,128]{2,1,0:T(8,128)}, f32[4,72,128]{2,1,0:T(8,128)S(1)}, u32[]{:S(2)}, u32[]{:S(2)}) %collective-permute-start.18) | collective-permute-done | bytes 147488 | tf_op jit(solution)/shard_map/ppermute | solution.py:339
  185.0 1.8 columns.13
  187.7 2.1 collective-permute-start.21
  189.8 10.1 %forward_inner.5 = (f32[256,128]{1,0:T(8,128)}, f32[256,128]{1,0:T(8,128)}, f32[2,72,128]{2,1,0:T(8,128)}, f32[2,72,128]{2,1,0:T(8,128)}, f32[8,128]{1,0:T(8,128)}) custom-call(s32[768]{0:T(1024)} %reshape.28.refs_0_, f32[256,128]{1,0:T(8,128)} %get-tuple-element.170.first.refs_1_, f32[256,128]{1,0:T(8,128)} %get-tuple-element.171.refs_2_, ...), custom_call_target="tpu_custom_call" | custom-call | flops 33554432 | bytes 3670016 | tf_op jit(solution)/shard_map/forward_inner/pallas_call | solution.py:268
  200.6 11.4 %forward_outer.5 = (f32[256,128]{1,0:T(8,128)}, f32[256,128]{1,0:T(8,128)}, f32[4,72,128]{2,1,0:T(8,128)}, f32[4,72,128]{2,1,0:T(8,128)}, f32[8,128]{1,0:T(8,128)}) custom-call(s32[768]{0:T(1024)} %reshape.28.refs_0_, f32[256,128]{1,0:T(8,128)} %get-tuple-element.170.first.refs_1_, f32[256,128]{1,0:T(8,128)} %get-tuple-element.171.refs_2_, ...), custom_call_target="tpu_custom_call" | custom-call | flops 33554432 | bytes 3670016 | tf_op jit(solution)/shard_map/forward_outer/pallas_call | solution.py:268
  212.1 3.5 %collective-permute-start.23 = (f32[4,72,128]{2,1,0:T(8,128)}, f32[4,72,128]{2,1,0:T(8,128)S(1)}, u32[]{:S(2)}, u32[]{:S(2)}) collective-permute-start(f32[4,72,128]{2,1,0:T(8,128)} %get-tuple-element.191), channel_id=1, source_target_pairs={{0,28},{4,0},{8,4},{12,8},{16,12},{20,16},{24,20},{28,24},{1,29},{... | collective-permute-start | bytes 442376 | tf_op jit(solution)/shard_map/ppermute | solution.py:339
  215.6 4.4 %collective-permute-done.22.top.refs_5_ = f32[4,72,128]{2,1,0:T(8,128)S(1)} collective-permute-done((f32[4,72,128]{2,1,0:T(8,128)}, f32[4,72,128]{2,1,0:T(8,128)S(1)}, u32[]{:S(2)}, u32[]{:S(2)}) %collective-permute-start.22) | collective-permute-done | bytes 147488 | tf_op jit(solution)/shard_map/ppermute | solution.py:339
  220.7 1.8 columns.14
  223.2 2.3 collective-permute-start.25
  225.5 10.0 %forward_inner.6 = (f32[256,128]{1,0:T(8,128)}, f32[256,128]{1,0:T(8,128)}, f32[2,72,128]{2,1,0:T(8,128)}, f32[2,72,128]{2,1,0:T(8,128)}, f32[8,128]{1,0:T(8,128)}) custom-call(s32[768]{0:T(1024)} %reshape.28.refs_0_, f32[256,128]{1,0:T(8,128)} %get-tuple-element.186.first.refs_1_, f32[256,128]{1,0:T(8,128)} %get-tuple-element.187.refs_2_, ...), custom_call_target="tpu_custom_call" | custom-call | flops 33554432 | bytes 3670016 | tf_op jit(solution)/shard_map/forward_inner/pallas_call | solution.py:268
  236.3 11.4 %forward_outer.6 = (f32[256,128]{1,0:T(8,128)}, f32[256,128]{1,0:T(8,128)}, f32[4,72,128]{2,1,0:T(8,128)}, f32[4,72,128]{2,1,0:T(8,128)}, f32[8,128]{1,0:T(8,128)}) custom-call(s32[768]{0:T(1024)} %reshape.28.refs_0_, f32[256,128]{1,0:T(8,128)} %get-tuple-element.186.first.refs_1_, f32[256,128]{1,0:T(8,128)} %get-tuple-element.187.refs_2_, ...), custom_call_target="tpu_custom_call" | custom-call | flops 33554432 | bytes 3670016 | tf_op jit(solution)/shard_map/forward_outer/pallas_call | solution.py:268
  247.8 3.5 %collective-permute-start.27 = (f32[4,72,128]{2,1,0:T(8,128)}, f32[4,72,128]{2,1,0:T(8,128)S(1)}, u32[]{:S(2)}, u32[]{:S(2)}) collective-permute-start(f32[4,72,128]{2,1,0:T(8,128)} %get-tuple-element.207), channel_id=1, source_target_pairs={{0,28},{4,0},{8,4},{12,8},{16,12},{20,16},{24,20},{28,24},{1,29},{... | collective-permute-start | bytes 442376 | tf_op jit(solution)/shard_map/ppermute | solution.py:339
  251.3 3.3 %collective-permute-done.26.top.refs_5_ = f32[4,72,128]{2,1,0:T(8,128)S(1)} collective-permute-done((f32[4,72,128]{2,1,0:T(8,128)}, f32[4,72,128]{2,1,0:T(8,128)S(1)}, u32[]{:S(2)}, u32[]{:S(2)}) %collective-permute-start.26) | collective-permute-done | bytes 147488 | tf_op jit(solution)/shard_map/ppermute | solution.py:339
  255.4 1.8 columns.15
  258.1 2.1 collective-permute-start.29
  260.2 10.0 %forward_inner.7 = (f32[256,128]{1,0:T(8,128)}, f32[256,128]{1,0:T(8,128)}, f32[2,72,128]{2,1,0:T(8,128)}, f32[2,72,128]{2,1,0:T(8,128)}, f32[8,128]{1,0:T(8,128)}) custom-call(s32[768]{0:T(1024)} %reshape.28.refs_0_, f32[256,128]{1,0:T(8,128)} %get-tuple-element.202.first.refs_1_, f32[256,128]{1,0:T(8,128)} %get-tuple-element.203.refs_2_, ...), custom_call_target="tpu_custom_call" | custom-call | flops 33554432 | bytes 3670016 | tf_op jit(solution)/shard_map/forward_inner/pallas_call | solution.py:268
  271.0 11.5 %forward_outer.7 = (f32[256,128]{1,0:T(8,128)}, f32[256,128]{1,0:T(8,128)}, f32[4,72,128]{2,1,0:T(8,128)}, f32[4,72,128]{2,1,0:T(8,128)}, f32[8,128]{1,0:T(8,128)}) custom-call(s32[768]{0:T(1024)} %reshape.28.refs_0_, f32[256,128]{1,0:T(8,128)} %get-tuple-element.202.first.refs_1_, f32[256,128]{1,0:T(8,128)} %get-tuple-element.203.refs_2_, ...), custom_call_target="tpu_custom_call" | custom-call | flops 33554432 | bytes 3670016 | tf_op jit(solution)/shard_map/forward_outer/pallas_call | solution.py:268
  287.0 2.4 collective-permute-done.32
  292.9 2.8 collective-permute-start.36
  (142 shorter events, 39.5 us)
Async XLA Ops:
  0.6 18.3 %copy-start.36 = (f32[4,8]{1,0:T(4,128)S(1)}, f32[4,8]{1,0:T(4,128)}, u32[]{:S(2)}) copy-start(f32[4,8]{1,0:T(4,128)} %param.11) | copy-start | bytes 388
  3.0 9.7 %collective-permute-start = (f32[8,72,128]{2,1,0:T(8,128)}, f32[8,72,128]{2,1,0:T(8,128)S(1)}, u32[]{:S(2)}, u32[]{:S(2)}) collective-permute-start(f32[8,72,128]{2,1,0:T(8,128)} %get-tuple-element.117), channel_id=1, source_target_pairs={{0,4},{4,8},{8,12},{12,16},{16,20},{20,24},{24,28},{28,0},{1,5},{5... | collective-permute-start | bytes 884744 | tf_op jit(solution)/shard_map/ppermute | solution.py:339
  3.5 9.7 %collective-permute-start.1 = (f32[8,72,128]{2,1,0:T(8,128)}, f32[8,72,128]{2,1,0:T(8,128)S(1)}, u32[]{:S(2)}, u32[]{:S(2)}) collective-permute-start(f32[8,72,128]{2,1,0:T(8,128)} %get-tuple-element.118), channel_id=1, source_target_pairs={{0,28},{4,0},{8,4},{12,8},{16,12},{20,16},{24,20},{28,24},{1,29},{... | collective-permute-start | bytes 884744 | tf_op jit(solution)/shard_map/ppermute | solution.py:339
  15.8 14.2 %collective-permute-start.2 = (f32[400,128]{1,0:T(8,128)}, f32[400,128]{1,0:T(8,128)S(1)}, u32[]{:S(2)}, u32[]{:S(2)}) collective-permute-start(f32[400,128]{1,0:T(8,128)} %get-tuple-element.119), channel_id=1, source_target_pairs={{0,1},{1,2},{2,3},{3,0},{4,5},{5,6},{6,7},{7,4},{8,9},{9,10},{10,1... | collective-permute-start | bytes 614408 | tf_op jit(solution)/shard_map/ppermute | solution.py:339
  17.9 12.1 %collective-permute-start.3 = (f32[400,128]{1,0:T(8,128)}, f32[400,128]{1,0:T(8,128)S(1)}, u32[]{:S(2)}, u32[]{:S(2)}) collective-permute-start(f32[400,128]{1,0:T(8,128)} %get-tuple-element.120), channel_id=1, source_target_pairs={{0,3},{1,0},{2,1},{3,2},{4,7},{5,4},{6,5},{7,6},{8,11},{9,8},{10,9... | collective-permute-start | bytes 614408 | tf_op jit(solution)/shard_map/ppermute | solution.py:339
  30.0 0.7 copy-start.29
  42.6 6.7 %collective-permute-start.4 = (f32[4,72,128]{2,1,0:T(8,128)}, f32[4,72,128]{2,1,0:T(8,128)S(1)}, u32[]{:S(2)}, u32[]{:S(2)}) collective-permute-start(f32[4,72,128]{2,1,0:T(8,128)} %get-tuple-element.127), channel_id=1, source_target_pairs={{0,4},{4,8},{8,12},{12,16},{16,20},{20,24},{24,28},{28,0},{1,5},{5... | collective-permute-start | bytes 442376 | tf_op jit(solution)/shard_map/ppermute | solution.py:339
  44.2 5.1 %collective-permute-start.5 = (f32[4,72,128]{2,1,0:T(8,128)}, f32[4,72,128]{2,1,0:T(8,128)S(1)}, u32[]{:S(2)}, u32[]{:S(2)}) collective-permute-start(f32[4,72,128]{2,1,0:T(8,128)} %get-tuple-element.128), channel_id=1, source_target_pairs={{0,28},{4,0},{8,4},{12,8},{16,12},{20,16},{24,20},{28,24},{1,29},{... | collective-permute-start | bytes 442376 | tf_op jit(solution)/shard_map/ppermute | solution.py:339
  51.9 13.5 %collective-permute-start.6 = (f32[400,128]{1,0:T(8,128)}, f32[400,128]{1,0:T(8,128)S(1)}, u32[]{:S(2)}, u32[]{:S(2)}) collective-permute-start(f32[400,128]{1,0:T(8,128)} %get-tuple-element.129), channel_id=1, source_target_pairs={{0,1},{1,2},{2,3},{3,0},{4,5},{5,6},{6,7},{7,4},{8,9},{9,10},{10,1... | collective-permute-start | bytes 614408 | tf_op jit(solution)/shard_map/ppermute | solution.py:339
  52.9 12.6 %collective-permute-start.7 = (f32[400,128]{1,0:T(8,128)}, f32[400,128]{1,0:T(8,128)S(1)}, u32[]{:S(2)}, u32[]{:S(2)}) collective-permute-start(f32[400,128]{1,0:T(8,128)} %get-tuple-element.130), channel_id=1, source_target_pairs={{0,3},{1,0},{2,1},{3,2},{4,7},{5,4},{6,5},{7,6},{8,11},{9,8},{10,9... | collective-permute-start | bytes 614408 | tf_op jit(solution)/shard_map/ppermute | solution.py:339
  78.1 7.5 %collective-permute-start.8 = (f32[4,72,128]{2,1,0:T(8,128)}, f32[4,72,128]{2,1,0:T(8,128)S(1)}, u32[]{:S(2)}, u32[]{:S(2)}) collective-permute-start(f32[4,72,128]{2,1,0:T(8,128)} %get-tuple-element.137), channel_id=1, source_target_pairs={{0,4},{4,8},{8,12},{12,16},{16,20},{20,24},{24,28},{28,0},{1,5},{5... | collective-permute-start | bytes 442376 | tf_op jit(solution)/shard_map/ppermute | solution.py:339
  78.6 6.9 %collective-permute-start.9 = (f32[4,72,128]{2,1,0:T(8,128)}, f32[4,72,128]{2,1,0:T(8,128)S(1)}, u32[]{:S(2)}, u32[]{:S(2)}) collective-permute-start(f32[4,72,128]{2,1,0:T(8,128)} %get-tuple-element.138), channel_id=1, source_target_pairs={{0,28},{4,0},{8,4},{12,8},{16,12},{20,16},{24,20},{28,24},{1,29},{... | collective-permute-start | bytes 442376 | tf_op jit(solution)/shard_map/ppermute | solution.py:339
  88.1 13.5 %collective-permute-start.10 = (f32[400,128]{1,0:T(8,128)}, f32[400,128]{1,0:T(8,128)S(1)}, u32[]{:S(2)}, u32[]{:S(2)}) collective-permute-start(f32[400,128]{1,0:T(8,128)} %get-tuple-element.139), channel_id=1, source_target_pairs={{0,1},{1,2},{2,3},{3,0},{4,5},{5,6},{6,7},{7,4},{8,9},{9,10},{10,1... | collective-permute-start | bytes 614408 | tf_op jit(solution)/shard_map/ppermute | solution.py:339
  89.3 12.3 %collective-permute-start.11 = (f32[400,128]{1,0:T(8,128)}, f32[400,128]{1,0:T(8,128)S(1)}, u32[]{:S(2)}, u32[]{:S(2)}) collective-permute-start(f32[400,128]{1,0:T(8,128)} %get-tuple-element.140), channel_id=1, source_target_pairs={{0,3},{1,0},{2,1},{3,2},{4,7},{5,4},{6,5},{7,6},{8,11},{9,8},{10,9... | collective-permute-start | bytes 614408 | tf_op jit(solution)/shard_map/ppermute | solution.py:339
  101.6 0.7 copy-start.27
  114.1 7.4 %collective-permute-start.12 = (f32[4,72,128]{2,1,0:T(8,128)}, f32[4,72,128]{2,1,0:T(8,128)S(1)}, u32[]{:S(2)}, u32[]{:S(2)}) collective-permute-start(f32[4,72,128]{2,1,0:T(8,128)} %get-tuple-element.147), channel_id=1, source_target_pairs={{0,4},{4,8},{8,12},{12,16},{16,20},{20,24},{24,28},{28,0},{1,5},{5... | collective-permute-start | bytes 442376 | tf_op jit(solution)/shard_map/ppermute | solution.py:339
  114.2 7.4 %collective-permute-start.13 = (f32[4,72,128]{2,1,0:T(8,128)}, f32[4,72,128]{2,1,0:T(8,128)S(1)}, u32[]{:S(2)}, u32[]{:S(2)}) collective-permute-start(f32[4,72,128]{2,1,0:T(8,128)} %get-tuple-element.148), channel_id=1, source_target_pairs={{0,28},{4,0},{8,4},{12,8},{16,12},{20,16},{24,20},{28,24},{1,29},{... | collective-permute-start | bytes 442376 | tf_op jit(solution)/shard_map/ppermute | solution.py:339
  124.1 28.5 %collective-permute-start.14 = (f32[400,128]{1,0:T(8,128)}, f32[400,128]{1,0:T(8,128)S(1)}, u32[]{:S(2)}, u32[]{:S(2)}) collective-permute-start(f32[400,128]{1,0:T(8,128)} %get-tuple-element.149), channel_id=1, source_target_pairs={{0,1},{1,2},{2,3},{3,0},{4,5},{5,6},{6,7},{7,4},{8,9},{9,10},{10,1... | collective-permute-start | bytes 614408 | tf_op jit(solution)/shard_map/ppermute | solution.py:339
  124.8 27.8 %collective-permute-start.15 = (f32[400,128]{1,0:T(8,128)}, f32[400,128]{1,0:T(8,128)S(1)}, u32[]{:S(2)}, u32[]{:S(2)}) collective-permute-start(f32[400,128]{1,0:T(8,128)} %get-tuple-element.150), channel_id=1, source_target_pairs={{0,3},{1,0},{2,1},{3,2},{4,7},{5,4},{6,5},{7,6},{8,11},{9,8},{10,9... | collective-permute-start | bytes 614408 | tf_op jit(solution)/shard_map/ppermute | solution.py:339
  129.0 36.2 %collective-permute-start.16 = (f32[400,128]{1,0:T(8,128)}, f32[400,128]{1,0:T(8,128)S(1)}, u32[]{:S(2)}, u32[]{:S(2)}) collective-permute-start(f32[400,128]{1,0:T(8,128)} %get-tuple-element.161), channel_id=1, source_target_pairs={{0,1},{1,2},{2,3},{3,0},{4,5},{5,6},{6,7},{7,4},{8,9},{9,10},{10,1... | collective-permute-start | bytes 614408 | tf_op jit(solution)/shard_map/ppermute | solution.py:339
  129.3 35.8 %collective-permute-start.17 = (f32[400,128]{1,0:T(8,128)}, f32[400,128]{1,0:T(8,128)S(1)}, u32[]{:S(2)}, u32[]{:S(2)}) collective-permute-start(f32[400,128]{1,0:T(8,128)} %get-tuple-element.162), channel_id=1, source_target_pairs={{0,3},{1,0},{2,1},{3,2},{4,7},{5,4},{6,5},{7,6},{8,11},{9,8},{10,9... | collective-permute-start | bytes 614408 | tf_op jit(solution)/shard_map/ppermute | solution.py:339
  152.6 0.7 copy-start.17
  165.2 0.8 copy-start.15
  177.3 6.9 %collective-permute-start.18 = (f32[4,72,128]{2,1,0:T(8,128)}, f32[4,72,128]{2,1,0:T(8,128)S(1)}, u32[]{:S(2)}, u32[]{:S(2)}) collective-permute-start(f32[4,72,128]{2,1,0:T(8,128)} %get-tuple-element.174), channel_id=1, source_target_pairs={{0,4},{4,8},{8,12},{12,16},{16,20},{20,24},{24,28},{28,0},{1,5},{5... | collective-permute-start | bytes 442376 | tf_op jit(solution)/shard_map/ppermute | solution.py:339
  177.4 6.9 %collective-permute-start.19 = (f32[4,72,128]{2,1,0:T(8,128)}, f32[4,72,128]{2,1,0:T(8,128)S(1)}, u32[]{:S(2)}, u32[]{:S(2)}) collective-permute-start(f32[4,72,128]{2,1,0:T(8,128)} %get-tuple-element.175), channel_id=1, source_target_pairs={{0,28},{4,0},{8,4},{12,8},{16,12},{20,16},{24,20},{28,24},{1,29},{... | collective-permute-start | bytes 442376 | tf_op jit(solution)/shard_map/ppermute | solution.py:339
  186.8 13.0 %collective-permute-start.20 = (f32[400,128]{1,0:T(8,128)}, f32[400,128]{1,0:T(8,128)S(1)}, u32[]{:S(2)}, u32[]{:S(2)}) collective-permute-start(f32[400,128]{1,0:T(8,128)} %get-tuple-element.176), channel_id=1, source_target_pairs={{0,1},{1,2},{2,3},{3,0},{4,5},{5,6},{6,7},{7,4},{8,9},{9,10},{10,1... | collective-permute-start | bytes 614408 | tf_op jit(solution)/shard_map/ppermute | solution.py:339
  187.7 12.2 %collective-permute-start.21 = (f32[400,128]{1,0:T(8,128)}, f32[400,128]{1,0:T(8,128)S(1)}, u32[]{:S(2)}, u32[]{:S(2)}) collective-permute-start(f32[400,128]{1,0:T(8,128)} %get-tuple-element.177), channel_id=1, source_target_pairs={{0,3},{1,0},{2,1},{3,2},{4,7},{5,4},{6,5},{7,6},{8,11},{9,8},{10,9... | collective-permute-start | bytes 614408 | tf_op jit(solution)/shard_map/ppermute | solution.py:339
  212.0 8.0 %collective-permute-start.22 = (f32[4,72,128]{2,1,0:T(8,128)}, f32[4,72,128]{2,1,0:T(8,128)S(1)}, u32[]{:S(2)}, u32[]{:S(2)}) collective-permute-start(f32[4,72,128]{2,1,0:T(8,128)} %get-tuple-element.190), channel_id=1, source_target_pairs={{0,4},{4,8},{8,12},{12,16},{16,20},{20,24},{24,28},{28,0},{1,5},{5... | collective-permute-start | bytes 442376 | tf_op jit(solution)/shard_map/ppermute | solution.py:339
  212.1 7.9 %collective-permute-start.23 = (f32[4,72,128]{2,1,0:T(8,128)}, f32[4,72,128]{2,1,0:T(8,128)S(1)}, u32[]{:S(2)}, u32[]{:S(2)}) collective-permute-start(f32[4,72,128]{2,1,0:T(8,128)} %get-tuple-element.191), channel_id=1, source_target_pairs={{0,28},{4,0},{8,4},{12,8},{16,12},{20,16},{24,20},{28,24},{1,29},{... | collective-permute-start | bytes 442376 | tf_op jit(solution)/shard_map/ppermute | solution.py:339
  222.6 13.0 %collective-permute-start.24 = (f32[400,128]{1,0:T(8,128)}, f32[400,128]{1,0:T(8,128)S(1)}, u32[]{:S(2)}, u32[]{:S(2)}) collective-permute-start(f32[400,128]{1,0:T(8,128)} %get-tuple-element.192), channel_id=1, source_target_pairs={{0,1},{1,2},{2,3},{3,0},{4,5},{5,6},{6,7},{7,4},{8,9},{9,10},{10,1... | collective-permute-start | bytes 614408 | tf_op jit(solution)/shard_map/ppermute | solution.py:339
  223.2 12.4 %collective-permute-start.25 = (f32[400,128]{1,0:T(8,128)}, f32[400,128]{1,0:T(8,128)S(1)}, u32[]{:S(2)}, u32[]{:S(2)}) collective-permute-start(f32[400,128]{1,0:T(8,128)} %get-tuple-element.193), channel_id=1, source_target_pairs={{0,3},{1,0},{2,1},{3,2},{4,7},{5,4},{6,5},{7,6},{8,11},{9,8},{10,9... | collective-permute-start | bytes 614408 | tf_op jit(solution)/shard_map/ppermute | solution.py:339
  247.8 6.9 %collective-permute-start.26 = (f32[4,72,128]{2,1,0:T(8,128)}, f32[4,72,128]{2,1,0:T(8,128)S(1)}, u32[]{:S(2)}, u32[]{:S(2)}) collective-permute-start(f32[4,72,128]{2,1,0:T(8,128)} %get-tuple-element.206), channel_id=1, source_target_pairs={{0,4},{4,8},{8,12},{12,16},{16,20},{20,24},{24,28},{28,0},{1,5},{5... | collective-permute-start | bytes 442376 | tf_op jit(solution)/shard_map/ppermute | solution.py:339
  247.8 6.9 %collective-permute-start.27 = (f32[4,72,128]{2,1,0:T(8,128)}, f32[4,72,128]{2,1,0:T(8,128)S(1)}, u32[]{:S(2)}, u32[]{:S(2)}) collective-permute-start(f32[4,72,128]{2,1,0:T(8,128)} %get-tuple-element.207), channel_id=1, source_target_pairs={{0,28},{4,0},{8,4},{12,8},{16,12},{20,16},{24,20},{28,24},{1,29},{... | collective-permute-start | bytes 442376 | tf_op jit(solution)/shard_map/ppermute | solution.py:339
  257.2 13.0 %collective-permute-start.28 = (f32[400,128]{1,0:T(8,128)}, f32[400,128]{1,0:T(8,128)S(1)}, u32[]{:S(2)}, u32[]{:S(2)}) collective-permute-start(f32[400,128]{1,0:T(8,128)} %get-tuple-element.208), channel_id=1, source_target_pairs={{0,1},{1,2},{2,3},{3,0},{4,5},{5,6},{6,7},{7,4},{8,9},{9,10},{10,1... | collective-permute-start | bytes 614408 | tf_op jit(solution)/shard_map/ppermute | solution.py:339
  258.1 12.1 %collective-permute-start.29 = (f32[400,128]{1,0:T(8,128)}, f32[400,128]{1,0:T(8,128)S(1)}, u32[]{:S(2)}, u32[]{:S(2)}) collective-permute-start(f32[400,128]{1,0:T(8,128)} %get-tuple-element.209), channel_id=1, source_target_pairs={{0,3},{1,0},{2,1},{3,2},{4,7},{5,4},{6,5},{7,6},{8,11},{9,8},{10,9... | collective-permute-start | bytes 614408 | tf_op jit(solution)/shard_map/ppermute | solution.py:339
  271.0 24.7 %copy-start.30 = (f32[256,128]{1,0:T(8,128)S(1)}, f32[256,128]{1,0:T(8,128)}, u32[]{:S(2)}) copy-start(f32[256,128]{1,0:T(8,128)} %get-tuple-element.154) | copy-start | bytes 393220
  271.0 24.7 %copy-start.31 = (f32[256,128]{1,0:T(8,128)S(1)}, f32[256,128]{1,0:T(8,128)}, u32[]{:S(2)}) copy-start(f32[256,128]{1,0:T(8,128)} %get-tuple-element.155) | copy-start | bytes 393220
  271.0 24.7 %copy-start.32 = (f32[256,128]{1,0:T(8,128)S(1)}, f32[256,128]{1,0:T(8,128)}, u32[]{:S(2)}) copy-start(f32[256,128]{1,0:T(8,128)} %get-tuple-element.153) | copy-start | bytes 393220
  271.0 24.7 %copy-start.33 = (f32[256,128]{1,0:T(8,128)S(1)}, f32[256,128]{1,0:T(8,128)}, u32[]{:S(2)}) copy-start(f32[256,128]{1,0:T(8,128)} %get-tuple-element.156) | copy-start | bytes 393220
  271.0 33.7 %copy-start.34 = (f32[256,128]{1,0:T(8,128)S(1)}, f32[256,128]{1,0:T(8,128)}, u32[]{:S(2)}) copy-start(f32[256,128]{1,0:T(8,128)} %get-tuple-element.219) | copy-start | bytes 393220
  271.0 33.7 %copy-start.35 = (f32[256,128]{1,0:T(8,128)S(1)}, f32[256,128]{1,0:T(8,128)}, u32[]{:S(2)}) copy-start(f32[256,128]{1,0:T(8,128)} %get-tuple-element.220) | copy-start | bytes 393220
  282.5 3.9 %collective-permute-start.30 = (f32[8,128]{1,0:T(8,128)}, f32[8,128]{1,0:T(8,128)S(1)}, u32[]{:S(2)}, u32[]{:S(2)}) collective-permute-start(f32[8,128]{1,0:T(8,128)} %get-tuple-element.222), channel_id=1, source_target_pairs={{0,1},{1,0},{2,3},{3,2},{4,5},{5,4},{6,7},{7,6},{8,9},{9,8},{10,11... | collective-permute-start | bytes 12296 | tf_op jit(solution)/shard_map/ppermute | solution.py:362
  283.2 3.8 %collective-permute-start.31 = (f32[8,128]{1,0:T(8,128)}, f32[8,128]{1,0:T(8,128)S(1)}, u32[]{:S(2)}, u32[]{:S(2)}) collective-permute-start(f32[8,128]{1,0:T(8,128)} %get-tuple-element.222), channel_id=1, source_target_pairs={{0,2},{1,3},{2,0},{3,1},{4,6},{5,7},{6,4},{7,5},{8,10},{9,11},{10,... | collective-permute-start | bytes 12296 | tf_op jit(solution)/shard_map/ppermute | solution.py:362
  284.7 4.7 %collective-permute-start.32 = (f32[8,128]{1,0:T(8,128)}, f32[8,128]{1,0:T(8,128)S(1)}, u32[]{:S(2)}, u32[]{:S(2)}) collective-permute-start(f32[8,128]{1,0:T(8,128)} %get-tuple-element.222), channel_id=1, source_target_pairs={{0,3},{1,2},{2,1},{3,0},{4,7},{5,6},{6,5},{7,4},{8,11},{9,10},{10,... | collective-permute-start | bytes 12296 | tf_op jit(solution)/shard_map/ppermute | solution.py:362
  290.1 1.2 collective-permute-start.33
  291.3 5.2 %collective-permute-start.34 = (f32[8,128]{1,0:T(8,128)S(1)}, f32[8,128]{1,0:T(8,128)S(1)}, u32[]{:S(2)}, u32[]{:S(2)}) collective-permute-start(f32[8,128]{1,0:T(8,128)S(1)} %add.135), channel_id=1, source_target_pairs={{0,8},{4,12},{8,0},{12,4},{16,24},{20,28},{24,16},{28,20},{1,9},{5... | collective-permute-start | bytes 12296 | tf_op jit(solution)/shard_map/ppermute | solution.py:362
  291.3 5.2 %collective-permute-start.35 = (f32[8,128]{1,0:T(8,128)S(1)}, f32[8,128]{1,0:T(8,128)S(1)}, u32[]{:S(2)}, u32[]{:S(2)}) collective-permute-start(f32[8,128]{1,0:T(8,128)S(1)} %add.135), channel_id=1, source_target_pairs={{0,16},{4,20},{8,24},{12,28},{16,0},{20,4},{24,8},{28,12},{1,17},{... | collective-permute-start | bytes 12296 | tf_op jit(solution)/shard_map/ppermute | solution.py:362
  292.9 5.4 %collective-permute-start.36 = (f32[8,128]{1,0:T(8,128)S(1)}, f32[8,128]{1,0:T(8,128)S(1)}, u32[]{:S(2)}, u32[]{:S(2)}) collective-permute-start(f32[8,128]{1,0:T(8,128)S(1)} %add.135), channel_id=1, source_target_pairs={{0,24},{4,28},{8,16},{12,20},{16,8},{20,12},{24,0},{28,4},{1,25},{... | collective-permute-start | bytes 12296 | tf_op jit(solution)/shard_map/ppermute | solution.py:362
  (26 other events, 18.0 us)
